TPU v7x, 512 devices: a whole 4x8x8 slice. The times are simulated.
512 devices in a mesh: region: 8 (over z_hi, core), shard: 64 (over z_lo, x, y).
Axes of the slice: x: 4, y: 8, z: 8 (z_hi: 4, z_lo: 2; z = z_hi * 2 + z_lo), core: 2. Of those that a mesh axis runs over, the one named last changes fastest.
Arguments:
- points: bfloat16 [49152, 8, 128], P(('region', 'shard')), may hold values from -12 to 12
- block_owner: int32 [49152, 1], P(('region', 'shard')), may hold values from 0 to 63; in each aligned block of 96 rows (0 to 95, 96 to 191, ...) at most 3 rows name the same one
- block_node: int32 [49152], P(('region', 'shard')), may hold values from 0 to 1
- queries: bfloat16 [131072, 128], P(('region', 'shard')), may hold values from -240 to 240
- w_in: bfloat16 [128, 768], replicated, may hold values from -0.5 to 0.5
- w_key: bfloat16 [768, 768], replicated, may hold values from -0.21875 to 0.21875
- w_value: bfloat16 [768, 768], replicated, may hold values from -0.21875 to 0.21875
- w_query: bfloat16 [128, 768], replicated, may hold values from -0.5 to 0.5
- w_out: bfloat16 [768, 128], replicated, may hold values from -0.21875 to 0.21875
Outputs:
- readout: bfloat16 [131072, 128], P(('region', 'shard'))
Inputs may be any that keep to these rules, and one draw needn't show every extreme that they name: `block_owner`: among the 96 blocks of one device no shard is named more than 3 times, and some device names one shard exactly 3 times.
All inputs are finite; a program needn't handle non-finite values.
Results may differ from a plain program's by a relative error of at most 0.018.
Values may be sent and summed in bfloat16 or wider, within the bound.
No kernel may reach another device: no remote copies, remote signals or barrier semaphores. Data moves between devices by JAX's collectives and lax.ppermute only.
A program may use at most 64 MiB of HBM per device.

v0:
```python
import math

import jax
import jax.numpy as jnp
from jax import lax
from jax.sharding import PartitionSpec as P

HEADS = 12
HEAD_DIM = 64
S_DEV = 2


def layer_norm(pooled):
    mean = jnp.mean(pooled, axis=-1, keepdims=True)
    centred = pooled - mean
    spread = jnp.mean(centred * centred, axis=-1, keepdims=True)
    return (centred * lax.rsqrt(spread + 1e-05)).astype(jnp.bfloat16)


def block_ranks(owner_shard, shard_count):
    onehot = (owner_shard[..., None] == jnp.arange(shard_count, dtype=jnp.int32)).astype(jnp.int32)
    before = jnp.cumsum(onehot, axis=-2) - onehot
    return jnp.sum(before * onehot, axis=-1)


def body(points, block_owner, block_node, queries, w_in, w_key, w_value, w_query, w_out):
    shard_count = lax.axis_size("shard")
    block_count, block_points, in_features = points.shape
    model_width = w_in.shape[1]
    capacity = max(2, 2 * block_count // shard_count)
    owner_shard = block_owner[:, 0]
    routing = lax.all_gather(
        jnp.stack([owner_shard, block_node], axis=1), "shard", axis=0, tiled=True
    )
    routing = routing.reshape(shard_count, block_count, 2)
    every_owner = routing[:, :, 0]
    every_node = routing[:, :, 1]
    this_shard = lax.axis_index("shard")
    position = jnp.arange(shard_count, dtype=jnp.int32)[:, None] * capacity + block_ranks(
        every_owner, shard_count
    )
    arrives_here = every_owner == this_shard
    node_onehot = (
        (every_node[..., None] == jnp.arange(S_DEV, dtype=jnp.int32)) & arrives_here[..., None]
    ).astype(jnp.float32)
    node_onehot = node_onehot.reshape(shard_count * block_count, S_DEV)
    slot_onehot = (
        position.reshape(-1)[:, None]
        == jnp.arange(shard_count * capacity, dtype=jnp.int32)[None, :]
    ).astype(jnp.float32)
    assign = jnp.dot(node_onehot.T, slot_onehot, precision=lax.Precision.HIGHEST)
    slot_index = owner_shard * capacity + block_ranks(owner_shard, shard_count)
    outgoing = (
        jnp.zeros((shard_count * capacity, block_points, in_features), points.dtype)
        .at[slot_index]
        .set(points)
    )
    outgoing = outgoing.reshape(shard_count, capacity, block_points, in_features)
    messages = jax.nn.gelu(
        jnp.einsum(
            "jkpc,cd->jkpd",
            lax.all_to_all(outgoing, "shard", split_axis=0, concat_axis=0, tiled=True),
            w_in,
            preferred_element_type=jnp.float32,
        )
    ).astype(jnp.bfloat16)
    per_slot = messages.reshape(shard_count * capacity, block_points * model_width)
    pooled = jnp.dot(assign.astype(jnp.bfloat16), per_slot, preferred_element_type=jnp.float32)
    pooled = jnp.sum(pooled.reshape(S_DEV, block_points, model_width), axis=1)
    normed = layer_norm(pooled)
    query_count = queries.shape[0]
    query_vec = jnp.dot(queries, w_query, preferred_element_type=jnp.float32).astype(jnp.bfloat16)
    query_heads = query_vec.reshape(query_count, HEADS, HEAD_DIM)
    score_scale = HEAD_DIM ** (-0.5)
    starting = (
        jnp.full((query_count, HEADS), -1e30, jnp.float32),
        jnp.zeros((query_count, HEADS), jnp.float32),
        jnp.zeros((query_count, HEADS, HEAD_DIM), jnp.float32),
    )
    key_rows = jnp.dot(normed, w_key, preferred_element_type=jnp.float32).astype(jnp.bfloat16)
    value_rows = jnp.dot(normed, w_value, preferred_element_type=jnp.float32).astype(jnp.bfloat16)
    anchor_rows = jnp.concatenate([key_rows, value_rows], axis=1)
    region_rows = lax.all_gather(anchor_rows, "shard", axis=0, tiled=True)
    key_values = lax.all_gather(region_rows, "region", axis=0, tiled=True)
    row_count = key_values.shape[0]
    step_rows = math.gcd(row_count, 256)

    def one_block(block_index, carried):
        peak_now, denominator, numerator = carried
        block_rows = lax.dynamic_slice_in_dim(key_values, block_index * step_rows, step_rows, 0)
        key_block = block_rows[:, :model_width].reshape(step_rows, HEADS, HEAD_DIM)
        value_block = block_rows[:, model_width:].reshape(step_rows, HEADS, HEAD_DIM)
        scores = (
            jnp.einsum("qhd,rhd->qhr", query_heads, key_block, preferred_element_type=jnp.float32)
            * score_scale
        )
        new_peak = jnp.maximum(peak_now, jnp.max(scores, axis=-1))
        rescale = jnp.exp(peak_now - new_peak)
        exponent = jnp.exp(scores - new_peak[..., None])
        denominator = denominator * rescale + jnp.sum(exponent, axis=-1)
        numerator = numerator * rescale[..., None] + jnp.einsum(
            "qhr,rhd->qhd",
            exponent.astype(jnp.bfloat16),
            value_block,
            preferred_element_type=jnp.float32,
        )
        return (new_peak, denominator, numerator)

    finished = lax.fori_loop(0, row_count // step_rows, one_block, starting)
    peak_final, denominator, numerator = finished
    attended = (
        (numerator / denominator[..., None]).astype(jnp.bfloat16).reshape(query_count, model_width)
    )
    return jnp.dot(attended, w_out, preferred_element_type=jnp.float32).astype(jnp.bfloat16)


def solution(mesh):
    return jax.shard_map(
        body,
        mesh=mesh,
        in_specs=(
            P(("region", "shard"), None, None),
            P(("region", "shard"), None),
            P(("region", "shard")),
            P(("region", "shard"), None),
            P(),
            P(),
            P(),
            P(),
            P(),
        ),
        out_specs=P(("region", "shard"), None),
        check_vma=False,
    )
```

profile of v0, /device:TPU:1, one launch (start us, length us, event | category | flops | bytes accessed | tf_op | source)
XLA Modules:
  0.0 421.8 jit_solution(3084942516669463617)
XLA Ops:
  6.5 0.8 fusion.38
  7.4 0.1 reduce_window_sum.23
  7.5 0.8 select_reduce_fusion
  8.4 0.7 fusion.42
  9.0 0.8 broadcast_in_dim.17
  9.8 10.1 %scatter_fusion = bf16[192,8,128]{2,1,0:T(8,128)(2,1)} fusion(bf16[192,8,128]{2,1,0:T(8,128)(2,1)} %broadcast_in_dim.17, s32[96]{0:T(128)S(1)} %fusion.42, bf16[96,8,128]{2,1,0:T(8,128)(2,1)} %param.11), kind=kCustom, calls=%fused_computation | custom fusion | bytes 590208 | tf_op jit(solution)/shard_map/scatter | solution.py:56
  19.9 12.9 %all-to-all-start = ((bf16[64,3,8,128]{3,2,1,0:T(8,128)(2,1)}), bf16[64,3,8,128]{3,2,1,0:T(8,128)(2,1)S(1)}, u32[]{:S(2)}, u32[]{:S(2)}) async-start(bf16[64,3,8,128]{3,2,1,0:T(8,128)(2,1)} %bitcast.7), calls=%async_computation | async-start | bytes 786432 | tf_op jit(solution)/shard_map/all_to_all | solution.py:62
  32.8 0.7 add_bitcast_fusion
  33.5 129.2 %all-gather = s32[64,96,2]{1,2,0:T(2,128)S(1)} all-gather(s32[1,96,2]{1,2,0:T(2,128)S(1)} %add_bitcast_fusion), channel_id=1, replica_groups=mesh['region'=8,'shard'=64] {'shard'}, dimensions={0}, use_global_device_ids=true | all-gather | bytes 49920 | tf_op jit(solution)/shard_map/all_gather | solution.py:32
  162.7 0.1 slice_reduce_fusion
  162.8 0.1 compare_reduce_fusion
  162.9 0.1 and.12
  163.0 0.1 eq.66
  163.1 0.1 copy.43
  163.2 3.3 fusion.27
  166.6 0.1 broadcast_add_fusion
  166.7 0.1 add.82
  166.8 0.8 fusion.34
  167.6 1.6 fusion.22
  169.3 0.7 fusion.43
  170.0 0.2 multiply_reduce_fusion
  170.2 0.3 convolution_convert_fusion.2
  170.5 0.3 convolution_convert_fusion.3
  170.9 124.8 %all-gather.1 = bf16[64,2,1536]{2,1,0:T(2,128)(2,1)S(1)} all-gather(bf16[1,2,1536]{2,1,0:T(2,128)(2,1)S(1)} %maximum_bitcast_fusion), channel_id=1, replica_groups=mesh['region'=8,'shard'=64] {'shard'}, dimensions={0}, use_global_device_ids=true | all-gather | bytes 399360 | tf_op jit(solution)/shard_map/all_gather | solution.py:83
  295.7 0.1 reshape.85
  295.9 0.9 copy.46
  296.9 0.2 convolution_convert_fusion
  297.1 0.2 copy.47
  297.3 103.8 %all-gather.4.cloned.1.call-done = bf16[1024,1536]{0,1:T(8,128)(2,1)} async-done(((bf16[128,1536]{0,1:T(8,128)(2,1)}), bf16[1024,1536]{0,1:T(8,128)(2,1)}) %all-gather.4.cloned.1.call-update) | async-done | bytes 3145744 | tf_op jit(solution)/shard_map/all_gather | solution.py:84
  401.1 12.8 %while.18 = (s32[]{:T(128)}, f32[256,12]{0,1:T(8,128)S(1)}, f32[256,12]{0,1:T(8,128)S(1)}, f32[256,12,64]{0,2,1:T(8,128)S(1)}, bf16[1024,1536]{0,1:T(8,128)(2,1)...) while((s32[]{:T(128)}, f32[256,12]{0,1:T(8,128)S(1)}, ...), condition=%wide.region_11.12_spmd.clone, body=%wide.region_8.11_spmd.clone.sunk | while | flops 208223232 | bytes 13959363 | solution.py:109
  401.1 1.2 fusion.68
  402.3 0.6 bitcast_reduce_fusion.2
  403.0 0.5 fusion.69
  403.5 0.8 fusion.71
  404.3 1.2 fusion.68
  405.5 0.6 bitcast_reduce_fusion.2
  406.2 0.5 fusion.69
  406.7 0.8 fusion.71
  407.5 1.2 fusion.68
  408.7 0.6 bitcast_reduce_fusion.2
  409.4 0.5 fusion.69
  409.9 0.8 fusion.71
  410.7 1.2 fusion.68
  411.9 0.6 bitcast_reduce_fusion.2
  412.5 0.5 fusion.69
  413.1 0.8 fusion.71
  413.9 0.1 divide_convert_fusion
  414.0 0.9 convolution_convert_fusion.1
  (35 shorter events, 0.4 us)
Async XLA Ops:
  6.5 163.6 %copy-start = (bf16[768,768]{1,0:T(8,128)(2,1)S(1)}, bf16[768,768]{1,0:T(8,128)(2,1)}, u32[]{:S(2)}) copy-start(bf16[768,768]{1,0:T(8,128)(2,1)} %param.17) | copy-start | bytes 3538948
  6.5 161.1 %copy-start.5 = (bf16[128,768]{1,0:T(8,128)(2,1)S(1)}, bf16[128,768]{1,0:T(8,128)(2,1)}, u32[]{:S(2)}) copy-start(bf16[128,768]{1,0:T(8,128)(2,1)} %param.15) | copy-start | bytes 589828
  19.9 147.8 %all-to-all-start = ((bf16[64,3,8,128]{3,2,1,0:T(8,128)(2,1)}), bf16[64,3,8,128]{3,2,1,0:T(8,128)(2,1)S(1)}, u32[]{:S(2)}, u32[]{:S(2)}) async-start(bf16[64,3,8,128]{3,2,1,0:T(8,128)(2,1)} %bitcast.7), calls=%async_computation | async-start | bytes 786432 | tf_op jit(solution)/shard_map/all_to_all | solution.py:62
  32.8 368.3 %all-gather.4.cloned.1.call-start = ((), (), s32[]{:S(2)}) async-start(), calls=%async_computation.1 | async-start | bytes 3538944 | tf_op jit(solution)/shard_map/all_gather | solution.py:84
  169.3 1.3 copy-start.4
  169.9 126.9 %copy-start.1 = (bf16[128,768]{1,0:T(8,128)(2,1)S(1)}, bf16[128,768]{1,0:T(8,128)(2,1)}, u32[]{:S(2)}) copy-start(bf16[128,768]{1,0:T(8,128)(2,1)} %param.18) | copy-start | bytes 589828
  170.0 126.9 %copy-start.3 = (bf16[256,128]{1,0:T(8,128)(2,1)S(1)}, bf16[256,128]{1,0:T(8,128)(2,1)}, u32[]{:S(2)}) copy-start(bf16[256,128]{1,0:T(8,128)(2,1)} %param.14) | copy-start | bytes 196612
  401.1 12.9 %copy-start.2 = (bf16[768,128]{1,0:T(8,128)(2,1)S(1)}, bf16[768,128]{1,0:T(8,128)(2,1)}, u32[]{:S(2)}) copy-start(bf16[768,128]{1,0:T(8,128)(2,1)} %param.19) | copy-start | bytes 589828
Sparse Core Ops, SparseCore 0:
  296.9 104.1 all-gather.3
where the time goes:
time: 423 us; the launch traced here: 422 us
  blocking collectives  254 us (60%)
  waiting for transfers between devices  104 us (25%)
  local copies, waits for them, and re-layouts  17.4 us (4%)
  between operations  13.6 us (3%)
  starting transfers between devices  12.9 us (3%)
  matrix products  10.5 us (2%)
  other arithmetic  9.21 us (2%)
    all_gather x1, blocking collectives, body(): lax.all_gather(jnp.stack([owner_shard, block_node], axis=1), 'shard', axi...  129 us
    all_gather x1, blocking collectives, body(): region_rows = lax.all_gather(anchor_rows, 'shard', axis=0, tiled=True)  125 us
    all_gather x1, waiting for transfers between devices, body(): key_values = lax.all_gather(region_rows, 'region', axis=0, tiled=True)  104 us
    all_to_all x1, starting transfers between devices, body(): lax.all_to_all(outgoing, 'shard', split_axis=0, concat_axis=0, tiled=True)  12.9 us
    scatter x1, local copies, waits for them, and re-layouts, body(): outgoing = jnp.zeros((shard_count * capacity, block_points, in_features),...  10.1 us
  transfers between devices with their start and end apart: 2, of which 1 were waited for; matrix products, arithmetic and copies ran while one was open for 1% of the time, Pallas kernels for 0%

commit v1 on v0

v1 whole, which is shorter than its diff:
```python
import functools

import jax
import jax.numpy as jnp
from jax import lax
from jax.experimental import pallas as pl
from jax.experimental.pallas import tpu as pltpu
from jax.sharding import Mesh
from jax.sharding import PartitionSpec as P

HEADS = 12
HEAD_DIM = 64
S_DEV = 2
AXES = ("z_hi", "core", "z_lo", "x", "y")
SHARD = ("z_lo", "x", "y")
BF16 = jnp.bfloat16
F32 = jnp.float32


def layer_norm(pooled):
    mean = jnp.mean(pooled, axis=-1, keepdims=True)
    centred = pooled - mean
    spread = jnp.mean(centred * centred, axis=-1, keepdims=True)
    return (centred * lax.rsqrt(spread + 1e-05)).astype(BF16)


def attention_kernel(queries, near, far, w_query, w_key, w_value, w_out, out, heads_out):
    group = 4 * HEAD_DIM
    anchors = (near[...], far[...])
    lane = lax.broadcasted_iota(jnp.int32, (1, group), 1) // HEAD_DIM
    for g in range(HEADS // 4):
        cols = slice(g * group, (g + 1) * group)
        q = jnp.dot(queries[...], w_query[:, cols], preferred_element_type=F32).astype(BF16)
        q = q * jnp.asarray(HEAD_DIM**-0.5, BF16)
        keys = [jnp.dot(a, w_key[:, cols], preferred_element_type=F32).astype(BF16) for a in anchors]
        values = [jnp.dot(a, w_value[:, cols], preferred_element_type=F32).astype(BF16) for a in anchors]
        result = jnp.zeros((q.shape[0], group), F32)
        for h in range(4):
            mine = lane == h
            q_head = jnp.where(mine, q, jnp.zeros_like(q))
            scores = [
                lax.dot_general(q_head, k, (((1,), (1,)), ((), ())), preferred_element_type=F32) for k in keys
            ]
            peak = jnp.maximum(
                jnp.max(scores[0], axis=-1, keepdims=True), jnp.max(scores[1], axis=-1, keepdims=True)
            )
            expo = [jnp.exp(s - peak) for s in scores]
            total = jnp.sum(expo[0], axis=-1, keepdims=True) + jnp.sum(expo[1], axis=-1, keepdims=True)
            summed = jnp.dot(expo[0].astype(BF16), values[0], preferred_element_type=F32)
            summed += jnp.dot(expo[1].astype(BF16), values[1], preferred_element_type=F32)
            result = jnp.where(mine, summed / total, result)
        heads_out[:, cols] = result.astype(BF16)
    out[...] = jnp.dot(heads_out[...], w_out[...], preferred_element_type=F32).astype(BF16)


def attention(queries, near, far, w_query, w_key, w_value, w_out):
    vmem = pl.BlockSpec(memory_space=pltpu.VMEM)
    return pl.pallas_call(
        attention_kernel,
        out_shape=jax.ShapeDtypeStruct((queries.shape[0], w_out.shape[1]), BF16),
        in_specs=[vmem] * 7,
        out_specs=vmem,
        scratch_shapes=[pltpu.VMEM((queries.shape[0], w_query.shape[1]), BF16)],
        compiler_params=pltpu.CompilerParams(vmem_limit_bytes=48 * 1024 * 1024),
        name="attention",
    )(queries, near, far, w_query, w_key, w_value, w_out)


def spread(rows, axes):
    count = lax.axis_size(axes)
    copies = jnp.broadcast_to(rows[None], (count, *rows.shape))
    return lax.all_to_all(copies, axes, 0, 0, tiled=True).reshape(-1, rows.shape[-1])


def body(points, block_owner, block_node, queries, w_in, w_key, w_value, w_query, w_out):
    shards = lax.axis_size(SHARD)
    block_count, block_points, in_features = points.shape
    width = w_in.shape[1]
    node = block_owner[:, 0] * S_DEV + block_node
    messages = jax.nn.gelu(
        jnp.dot(points.reshape(-1, in_features), w_in, preferred_element_type=F32)
    ).astype(BF16)
    pick = jnp.repeat(node, block_points)[None, :] == jnp.arange(shards * S_DEV, dtype=jnp.int32)[:, None]
    partial = jnp.dot(pick.astype(BF16), messages, preferred_element_type=F32).astype(BF16)
    arrived = lax.all_to_all(partial.reshape(shards, S_DEV, width), SHARD, 0, 0, tiled=True)
    normed = layer_norm(jnp.sum(arrived.astype(F32), axis=0))
    column = spread(normed, ("z_hi", "z_lo", "y"))
    near = spread(column, ("x",))
    far = lax.ppermute(near, "core", [(0, 1), (1, 0)])
    return attention(queries, near, far, w_query, w_key, w_value, w_out)


def solution(mesh):
    sizes = (mesh.shape["region"] // 2, 2, 2, 4, mesh.shape["shard"] // 8)
    fine = Mesh(mesh.devices.reshape(sizes), AXES)
    rows = P(AXES)
    return jax.shard_map(
        body,
        mesh=fine,
        in_specs=(rows, rows, rows, rows, P(), P(), P(), P(), P()),
        out_specs=rows,
        check_vma=False,
    )
```

time: 423 us -> 79.8 us (0.19)
  blocking collectives: 254 us -> 59.5 us
  waiting for transfers between devices: 104 us -> 1.89 us
  local copies, waits for them, and re-layouts: 17.4 us -> 0.58 us
  between operations: 13.6 us -> 0.1 us
  matrix products: 10.5 us -> 2.03 us
  Pallas kernels: 0 us -> 8.08 us
  other arithmetic: 9.21 us -> 1.52 us
  starting transfers between devices: 12.9 us -> 5.86 us
    all_gather x2 -> x0, blocking collectives: 254 us -> none  [the longest x1 129 us: body(): lax.all_gather(jnp.stack([owner_shard, block_node], axis=1), 'shard', axi...]
    all_gather x1 -> x0, waiting for transfers between devices: 104 us -> none  [body(): key_values = lax.all_gather(region_rows, 'region', axis=0, tiled=True)]
    all_to_all x0 -> x3, blocking collectives: none -> 59.5 us  [the longest x2 36.1 us: spread(): lax.all_to_all(copies, axes, 0, 0, tiled=True).reshape(-1, rows.shape[-1])]
    all_to_all x1 -> x0, starting transfers between devices: 12.9 us -> none  [body(): lax.all_to_all(outgoing, 'shard', split_axis=0, concat_axis=0, tiled=True)]
    scatter x1 -> x0, local copies, waits for them, and re-layouts: 10.1 us -> none  [body(): outgoing = jnp.zeros((shard_count * capacity, block_points, in_features),...]
    dot_general x15 -> x1, matrix products: 10.5 us -> 2.03 us  [body(): jnp.dot(pick.astype(BF16), messages, preferred_element_type=F32)]
    pallas_call x0 -> x1, Pallas kernels: none -> 8.08 us  [attention(): pl.pallas_call(attention_kernel, out_shape=jax.ShapeDtypeStruct((queries....]
    ppermute x0 -> x1, starting transfers between devices: none -> 5.86 us  [body(): far = lax.ppermute(near, 'core', [(0, 1), (1, 0)])]
  transfers between devices with their start and end apart: 2 -> 1, of which waited for: 1 -> 1; matrix products, arithmetic and copies ran while one was open for 1% -> 0% of each run, Pallas kernels for 0% -> 0%
where the time goes in v1:
time: 79.8 us; the launch traced here: 79.6 us
  blocking collectives  59.5 us (75%)
  Pallas kernels  8.08 us (10%)
  starting transfers between devices  5.86 us (7%)
  matrix products  2.03 us (3%)
  waiting for transfers between devices  1.89 us (2%)
  other arithmetic  1.52 us (2%)
    all_to_all x2, blocking collectives, spread(): lax.all_to_all(copies, axes, 0, 0, tiled=True).reshape(-1, rows.shape[-1])  36.1 us
    all_to_all x1, blocking collectives, body(): lax.all_to_all(partial.reshape(shards, S_DEV, width), SHARD, 0, 0, tiled=...  23.5 us
    pallas_call x1, Pallas kernels, attention(): pl.pallas_call(attention_kernel, out_shape=jax.ShapeDtypeStruct((queries....  8.08 us
    ppermute x1, starting transfers between devices, body(): far = lax.ppermute(near, 'core', [(0, 1), (1, 0)])  5.86 us
    dot_general x1, matrix products, body(): jnp.dot(pick.astype(BF16), messages, preferred_element_type=F32)  2.03 us
    ppermute x1, waiting for transfers between devices, body(): far = lax.ppermute(near, 'core', [(0, 1), (1, 0)])  1.89 us
  transfers between devices with their start and end apart: 1, of which 1 were waited for; matrix products, arithmetic and copies ran while one was open for 0% of the time, Pallas kernels for 0%

profile of v1, /device:TPU:1, one launch (start us, length us, event | category | flops | bytes accessed | tf_op | source)
XLA Modules:
  0.0 79.6 jit_solution(8191422727364112629)
XLA Ops:
  0.0 0.0 copy-start
  0.0 0.7 bitcast_add_fusion
  0.7 0.1 broadcast_in_dim.8
  0.8 0.1 eq.15
  0.9 0.1 copy-done
  1.0 2.0 %fusion.13 = bf16[128,768]{1,0:T(8,128)(2,1)S(1)} fusion(bf16[128,768]{1,0:T(8,128)(2,1)S(1)} %copy-done, bf16[96,8,128]{2,1,0:T(8,128)(2,1)} %param.9, s32[768]{0:T(1024)S(1)} %eq.15), kind=kOutput, calls=%fused_computation.14 | convolution fusion | flops 307494912 | bytes 592896 | tf_op jit(solution)/shard_map/dot_general | solution.py:84
  3.0 0.1 reshape.55
  3.1 23.5 %all_to_all.15 = bf16[64,2,768]{2,1,0:T(2,128)(2,1)S(1)} all-to-all(bf16[64,2,768]{2,1,0:T(2,128)(2,1)S(1)} %reshape.55), channel_id=1, replica_groups=mesh['z_hi'=4,'core'=2,'z_lo'=2,'x'=4,'y'=8] {'z_lo','x','y'}, dimensions={0} | all-to-all | bytes 393216 | tf_op jit(solution)/shard_map/all_to_all | solution.py:85
  26.5 0.5 convert_reduce_fusion
  27.1 0.2 multiply_reduce_fusion
  27.3 0.1 multiply_convert_fusion
  27.4 0.1 broadcast_in_dim.9
  27.5 24.2 %all_to_all.16 = bf16[64,2,768]{2,1,0:T(2,128)(2,1)S(1)} all-to-all(bf16[64,2,768]{2,1,0:T(2,128)(2,1)S(1)} %broadcast_in_dim.9), channel_id=1, replica_groups=mesh['z_hi'=4,'core'=2,'z_lo'=2,'x'=4,'y'=8] {'z_hi','z_lo','y'}, dimensions={0} | all-to-all | bytes 393216 | tf_op jit(solution)/shard_map/all_to_all | solution.py:72
  51.7 0.0 copy-start.4
  51.7 0.0 copy-start.5
  51.7 0.1 broadcast_in_dim.10
  51.8 0.0 copy-start.1
  51.8 0.0 copy-start.2
  51.8 0.0 copy-start.3
  51.8 0.1 broadcast_in_dim.22
  51.9 11.8 %all_to_all.17 = bf16[4,128,768]{2,1,0:T(8,128)(2,1)S(1)} all-to-all(bf16[4,128,768]{2,1,0:T(8,128)(2,1)S(1)} %broadcast_in_dim.22), channel_id=1, replica_groups=mesh['z_hi'=4,'core'=2,'z_lo'=2,'x'=4,'y'=8] {'x'}, dimensions={0} | all-to-all | bytes 1572864 | tf_op jit(solution)/shard_map/all_to_all | solution.py:72
  63.7 5.9 %collective-permute-start = (bf16[512,768]{1,0:T(8,128)(2,1)S(1)}, bf16[512,768]{1,0:T(8,128)(2,1)S(1)}, u32[]{:S(2)}, u32[]{:S(2)}) collective-permute-start(bf16[512,768]{1,0:T(8,128)(2,1)S(1)} %bitcast.8), channel_id=1, source_target_pairs={{0,64},{64,0},{1,65},{65,1},{2,66},{66,2},{3,67},{67,3},{4,68},{68... | collective-permute-start | bytes 2359304 | tf_op jit(solution)/shard_map/ppermute | solution.py:89
  69.6 1.9 %collective-permute-done.far = bf16[512,768]{1,0:T(8,128)(2,1)S(1)} collective-permute-done((bf16[512,768]{1,0:T(8,128)(2,1)S(1)}, bf16[512,768]{1,0:T(8,128)(2,1)S(1)}, u32[]{:S(2)}, u32[]{:S(2)}) %collective-permute-start) | collective-permute-done | bytes 786464 | tf_op jit(solution)/shard_map/ppermute | solution.py:89
  71.5 0.0 copy-done.4
  71.5 0.0 copy-done.5
  71.5 0.0 copy-done.1
  71.5 0.0 copy-done.2
  71.5 0.0 copy-done.3
  71.5 8.1 %attention.1 = bf16[256,128]{1,0:T(8,128)(2,1)} custom-call(bf16[256,128]{1,0:T(8,128)(2,1)S(1)} %copy-done.5, bf16[512,768]{1,0:T(8,128)(2,1)S(1)} %bitcast.9, bf16[512,768]{1,0:T(8,128)(2,1)S(1)} %collective-permute-done.far, bf16[128,768]{1,0:T(8,128)(2,1)S(1)} %copy-done.3, bf16[768,768]{1,0:T(8,128)(2,1)S(1)} %copy-done.1, ...), custom_call_target="tpu_custom_call" | custom-call | tf_op jit(solution)/shard_map/attention/pallas_call | solution.py:58
  (2 shorter events, 0.0 us)
Async XLA Ops:
  0.0 1.0 %copy-start = (bf16[128,768]{1,0:T(8,128)(2,1)S(1)}, bf16[128,768]{1,0:T(8,128)(2,1)}, u32[]{:S(2)}) copy-start(bf16[128,768]{1,0:T(8,128)(2,1)} %param.13) | copy-start | bytes 589828
  51.7 19.8 %copy-start.4 = (bf16[768,128]{1,0:T(8,128)(2,1)S(1)}, bf16[768,128]{1,0:T(8,128)(2,1)}, u32[]{:S(2)}) copy-start(bf16[768,128]{1,0:T(8,128)(2,1)} %w_out.1) | copy-start | bytes 589828
  51.7 19.8 %copy-start.5 = (bf16[256,128]{1,0:T(8,128)(2,1)S(1)}, bf16[256,128]{1,0:T(8,128)(2,1)}, u32[]{:S(2)}) copy-start(bf16[256,128]{1,0:T(8,128)(2,1)} %queries.1) | copy-start | bytes 196612
  51.8 19.7 %copy-start.1 = (bf16[768,768]{1,0:T(8,128)(2,1)S(1)}, bf16[768,768]{1,0:T(8,128)(2,1)}, u32[]{:S(2)}) copy-start(bf16[768,768]{1,0:T(8,128)(2,1)} %w_key.1) | copy-start | bytes 3538948
  51.8 19.7 %copy-start.2 = (bf16[768,768]{1,0:T(8,128)(2,1)S(1)}, bf16[768,768]{1,0:T(8,128)(2,1)}, u32[]{:S(2)}) copy-start(bf16[768,768]{1,0:T(8,128)(2,1)} %w_value.1) | copy-start | bytes 3538948
  51.8 19.7 %copy-start.3 = (bf16[128,768]{1,0:T(8,128)(2,1)S(1)}, bf16[128,768]{1,0:T(8,128)(2,1)}, u32[]{:S(2)}) copy-start(bf16[128,768]{1,0:T(8,128)(2,1)} %w_query.1) | copy-start | bytes 589828
  63.7 7.8 %collective-permute-start = (bf16[512,768]{1,0:T(8,128)(2,1)S(1)}, bf16[512,768]{1,0:T(8,128)(2,1)S(1)}, u32[]{:S(2)}, u32[]{:S(2)}) collective-permute-start(bf16[512,768]{1,0:T(8,128)(2,1)S(1)} %bitcast.8), channel_id=1, source_target_pairs={{0,64},{64,0},{1,65},{65,1},{2,66},{66,2},{3,67},{67,3},{4,68},{68... | collective-permute-start | bytes 2359304 | tf_op jit(solution)/shard_map/ppermute | solution.py:89

commit v2 on v1

v2 whole, which is shorter than its diff:
```python
import functools

import jax
import jax.numpy as jnp
from jax import lax
from jax.experimental import pallas as pl
from jax.experimental.pallas import tpu as pltpu
from jax.sharding import Mesh
from jax.sharding import PartitionSpec as P

HEADS = 12
HEAD_DIM = 64
S_DEV = 2
GROUP = 4 * HEAD_DIM
AXES = ("z_hi", "core", "z_lo", "x", "y")
SHARD = ("z_lo", "x", "y")
BF16 = jnp.bfloat16
F32 = jnp.float32
VMEM = pl.BlockSpec(memory_space=pltpu.VMEM)
SMEM = pl.BlockSpec(memory_space=pltpu.SMEM)


def matmul(a, b, dims=((1,), (0,))):
    return lax.dot_general(a, b, (dims, ((), ())), preferred_element_type=F32)


def layer_norm(pooled):
    mean = jnp.mean(pooled, axis=-1, keepdims=True)
    centred = pooled - mean
    spread = jnp.mean(centred * centred, axis=-1, keepdims=True)
    return (centred * lax.rsqrt(spread + 1e-05)).astype(BF16)


def pool_kernel(block_points, owner, node, points, w_in, out, pick):
    blocks = owner.shape[0]
    rows = 2 * block_points
    slots = out.shape[0]
    lane = lax.broadcasted_iota(jnp.int32, (rows, slots), 1)
    first = lax.broadcasted_iota(jnp.int32, (rows, slots), 0) < block_points
    for pair in range(blocks // 2):
        ids = [owner[b] * S_DEV + node[b] for b in (2 * pair, 2 * pair + 1)]
        chosen = lane == jnp.where(first, ids[0], ids[1])
        pick[rows * pair : rows * (pair + 1), :] = jnp.where(chosen, 1.0, 0.0).astype(BF16)
    for g in range(w_in.shape[1] // GROUP):
        cols = slice(g * GROUP, (g + 1) * GROUP)
        messages = jax.nn.gelu(matmul(points[...], w_in[:, cols])).astype(BF16)
        out[:, cols] = matmul(pick[...], messages, ((0,), (0,))).astype(BF16)


def pool(points, owner, node, w_in, slots):
    blocks, block_points, features = points.shape
    rows = blocks * block_points
    return pl.pallas_call(
        functools.partial(pool_kernel, block_points),
        out_shape=jax.ShapeDtypeStruct((slots, w_in.shape[1]), BF16),
        in_specs=[SMEM, SMEM, VMEM, VMEM],
        out_specs=VMEM,
        scratch_shapes=[pltpu.VMEM((rows, slots), BF16)],
        compiler_params=pltpu.CompilerParams(vmem_limit_bytes=16 * 1024 * 1024),
        cost_estimate=pl.CostEstimate(flops=2**28, bytes_accessed=2**20, transcendentals=2**19),
        name="pool",
    )(owner, node, points.reshape(rows, features), w_in)


def attend(q, anchors, w_key, w_value, old, store):
    lane = lax.broadcasted_iota(jnp.int32, (1, GROUP), 1) // HEAD_DIM
    for g in range(HEADS // 4):
        cols = slice(g * GROUP, (g + 1) * GROUP)
        q_group = q[:, cols]
        keys = [matmul(a, w_key[:, cols]).astype(BF16) for a in anchors]
        values = [matmul(a, w_value[:, cols]).astype(BF16) for a in anchors]
        peaks, totals, shrinks, result = [], [], [], None
        for h in range(4):
            mine = lane == h
            q_head = jnp.where(mine, q_group, jnp.zeros_like(q_group))
            scores = [matmul(q_head, k, ((1,), (1,))) for k in keys]
            peak = functools.reduce(jnp.maximum, [jnp.max(s, axis=-1, keepdims=True) for s in scores])
            before = old(g * 4 + h)
            if before is not None:
                peak = jnp.maximum(peak, before[0])
            expo = [jnp.exp(s - peak) for s in scores]
            total = sum(jnp.sum(e, axis=-1, keepdims=True) for e in expo)
            summed = sum(matmul(e.astype(BF16), v) for e, v in zip(expo, values))
            if before is not None:
                shrink = jnp.exp(before[0] - peak)
                total = total + before[1] * shrink
                shrinks.append(shrink)
            peaks.append(peak)
            totals.append(total)
            result = summed if result is None else jnp.where(mine, summed, result)
        store(g, cols, peaks, totals, shrinks, result, lane)


def by_head(parts, lane):
    wide = jnp.broadcast_to(parts[0], (parts[0].shape[0], GROUP))
    for h in range(1, 4):
        wide = jnp.where(lane == h, parts[h], wide)
    return wide


def first_kernel(queries, w_query, own, other, w_key, w_value, q, stats, summed):
    q[...] = (matmul(queries[...], w_query[...]).astype(BF16)) * jnp.asarray(HEAD_DIM**-0.5, BF16)

    def store(g, cols, peaks, totals, shrinks, result, lane):
        for h in range(4):
            stats[:, g * 4 + h : g * 4 + h + 1] = peaks[h]
            stats[:, 64 + g * 4 + h : 64 + g * 4 + h + 1] = totals[h]
        summed[:, cols] = result

    attend(q, [own[...], other[...]], w_key, w_value, lambda head: None, store)


def picked(place, rows):
    return [rows[lax.rem(place[0] + i, rows.shape[0])] for i in range(1, rows.shape[0])]


def next_kernel(place, q, rows, w_key, w_value, stats, summed, new_stats, new_summed):
    def old(head):
        return stats[:, head : head + 1], stats[:, 64 + head : 65 + head]

    def store(g, cols, peaks, totals, shrinks, result, lane):
        for h in range(4):
            new_stats[:, g * 4 + h : g * 4 + h + 1] = peaks[h]
            new_stats[:, 64 + g * 4 + h : 64 + g * 4 + h + 1] = totals[h]
        new_summed[:, cols] = result + summed[:, cols] * by_head(shrinks, lane)

    attend(q, picked(place, rows), w_key, w_value, old, store)


def last_kernel(place, q, rows, w_key, w_value, stats, summed, w_out, out, heads_out):
    def old(head):
        return stats[:, head : head + 1], stats[:, 64 + head : 65 + head]

    def store(g, cols, peaks, totals, shrinks, result, lane):
        full = result + summed[:, cols] * by_head(shrinks, lane)
        heads_out[:, cols] = (full / by_head(totals, lane)).astype(BF16)

    attend(q, picked(place, rows), w_key, w_value, old, store)
    out[...] = matmul(heads_out[...], w_out[...]).astype(BF16)


def cost(queries, anchors):
    return pl.CostEstimate(
        flops=anchors * 768 * 768 * 4 + queries * anchors * 768 * 16,
        bytes_accessed=2**20,
        transcendentals=queries * anchors * HEADS,
    )


def spread(rows, axes):
    count = lax.axis_size(axes)
    copies = jnp.broadcast_to(rows[None], (count, *rows.shape))
    return lax.all_to_all(copies, axes, 0, 0, tiled=True)


def swap(rows):
    return lax.ppermute(rows, "core", [(0, 1), (1, 0)])


def attention(queries, column, w_query, w_key, w_value, w_out):
    count, width = queries.shape[0], w_query.shape[1]
    place = lax.axis_index("x").reshape(1)
    params = pltpu.CompilerParams(vmem_limit_bytes=20 * 1024 * 1024)
    state = [
        jax.ShapeDtypeStruct((count, 128), F32),
        jax.ShapeDtypeStruct((count, width), F32),
    ]
    near = spread(column, ("x",))
    other = swap(column)
    first = pl.pallas_call(
        first_kernel,
        out_shape=[jax.ShapeDtypeStruct((count, width), BF16), *state],
        in_specs=[VMEM] * 6,
        out_specs=[VMEM] * 3,
        compiler_params=params,
        cost_estimate=cost(count, 2 * column.shape[0]),
        name="attend_first",
    )(queries, w_query, column, other, w_key, w_value)
    q, stats, summed = first
    far = swap(near)
    stats, summed = pl.pallas_call(
        next_kernel,
        out_shape=state,
        in_specs=[SMEM] + [VMEM] * 6,
        out_specs=[VMEM] * 2,
        compiler_params=params,
        cost_estimate=cost(count, 3 * column.shape[0]),
        name="attend_next",
    )(place, q, near, w_key, w_value, stats, summed)
    return pl.pallas_call(
        last_kernel,
        out_shape=jax.ShapeDtypeStruct((count, w_out.shape[1]), BF16),
        in_specs=[SMEM] + [VMEM] * 7,
        out_specs=VMEM,
        scratch_shapes=[pltpu.VMEM((count, width), BF16)],
        compiler_params=params,
        cost_estimate=cost(count, 3 * column.shape[0]),
        name="attend_last",
    )(place, q, far, w_key, w_value, stats, summed, w_out)


def body(points, block_owner, block_node, queries, w_in, w_key, w_value, w_query, w_out):
    shards = lax.axis_size(SHARD)
    width = w_in.shape[1]
    partial = pool(points, block_owner[:, 0], block_node, w_in, shards * S_DEV)
    arrived = lax.all_to_all(partial.reshape(shards, S_DEV, width), SHARD, 0, 0, tiled=True)
    normed = layer_norm(jnp.sum(arrived.astype(F32), axis=0))
    column = spread(normed, ("z_hi", "z_lo", "y")).reshape(-1, width)
    return attention(queries, column, w_query, w_key, w_value, w_out)


def solution(mesh):
    sizes = (mesh.shape["region"] // 2, 2, 2, 4, mesh.shape["shard"] // 8)
    fine = Mesh(mesh.devices.reshape(sizes), AXES)
    rows = P(AXES)
    return jax.shard_map(
        body,
        mesh=fine,
        in_specs=(rows, rows, rows, rows, P(), P(), P(), P(), P()),
        out_specs=rows,
        check_vma=False,
    )
```

time: 79.8 us -> 101 us (1.27)
  Pallas kernels: 8.08 us -> 26.7 us
  local copies, waits for them, and re-layouts: 0.58 us -> 4.34 us
  starting transfers between devices: 5.86 us -> 7.96 us
  matrix products: 2.03 us -> 0 us
    pallas_call x1 -> x4, Pallas kernels: 8.08 us -> 26.7 us  [the longest x1 10.7 us: attention(): pl.pallas_call(last_kernel, out_shape=jax.ShapeDtypeStruct((count, w_out....]
    unnamed x12 -> x18, local copies, waits for them, and re-layouts: 0.1 us -> 4.02 us
    ppermute x1 -> x2, starting transfers between devices: 5.86 us -> 7.96 us  [swap(): return lax.ppermute(rows, 'core', [(0, 1), (1, 0)])]
    dot_general x1 -> x0, matrix products: 2.03 us -> none  [body(): jnp.dot(pick.astype(BF16), messages, preferred_element_type=F32)]
  transfers between devices with their start and end apart: 1 -> 2, of which waited for: 1 -> 1; matrix products, arithmetic and copies ran while one was open for 0% -> 0% of each run, Pallas kernels for 0% -> 14%
where the time goes in v2:
time: 101 us
  blocking collectives  59.5 us (59%)
  Pallas kernels  26.7 us (26%)
  starting transfers between devices  7.96 us (8%)
  local copies, waits for them, and re-layouts  4.34 us (4%)
  waiting for transfers between devices  1.36 us (1%)
    all_to_all x2, blocking collectives, spread(): return lax.all_to_all(copies, axes, 0, 0, tiled=True)  36.1 us
    all_to_all x1, blocking collectives, body(): lax.all_to_all(partial.reshape(shards, S_DEV, width), SHARD, 0, 0, tiled=...  23.5 us
    pallas_call x1, Pallas kernels, attention(): pl.pallas_call(last_kernel, out_shape=jax.ShapeDtypeStruct((count, w_out....  10.7 us
    pallas_call x1, Pallas kernels, attention(): pl.pallas_call(next_kernel, out_shape=state, in_specs=[SMEM] + [VMEM] * 6...  9.83 us
    ppermute x2, starting transfers between devices, swap(): return lax.ppermute(rows, 'core', [(0, 1), (1, 0)])  7.96 us
    pallas_call x1, Pallas kernels, attention(): pl.pallas_call(first_kernel, out_shape=[jax.ShapeDtypeStruct((count, widt...  4.25 us
    unnamed x18, local copies, waits for them, and re-layouts  4.02 us
  transfers between devices with their start and end apart: 2, of which 1 were waited for; matrix products, arithmetic and copies ran while one was open for 0% of the time, Pallas kernels for 14%

profile of v2, /device:TPU:1, one launch (start us, length us, event | category | flops | bytes accessed | tf_op | source)
XLA Modules:
  0.0 100.9 jit_solution(13011822587361640775)
XLA Ops:
  0.0 0.0 copy-start.2
  0.0 0.9 copy-done.2
  0.9 0.0 copy-start.3
  0.9 0.9 copy-done.3
  1.9 0.0 copy-start.7
  1.9 0.7 copy-done.7
  2.5 0.0 copy-start.8
  2.5 0.7 copy-done.8
  3.2 2.0 %pool.1 = bf16[128,768]{1,0:T(8,128)(2,1)S(1)} custom-call(s32[96]{0:T(128)S(1)} %bitcast.4, s32[96]{0:T(128)S(1)} %copy-done.8, bf16[768,128]{1,0:T(8,128)(2,1)S(1)} %bitcast.3, bf16[128,768]{1,0:T(8,128)(2,1)S(1)} %copy-done.3), custom_call_target="tpu_custom_call" | custom-call | flops 268435456 | bytes 1048576 | tf_op jit(solution)/shard_map/pool/pallas_call | solution.py:53
  5.1 0.1 reshape.56
  5.2 23.5 %all_to_all.15 = bf16[64,2,768]{2,1,0:T(2,128)(2,1)S(1)} all-to-all(bf16[64,2,768]{2,1,0:T(2,128)(2,1)S(1)} %reshape.56), channel_id=1, replica_groups=mesh['z_hi'=4,'core'=2,'z_lo'=2,'x'=4,'y'=8] {'z_lo','x','y'}, dimensions={0} | all-to-all | bytes 393216 | tf_op jit(solution)/shard_map/all_to_all | solution.py:206
  28.7 0.5 convert_reduce_fusion
  29.2 0.2 multiply_reduce_fusion
  29.4 0.1 multiply_convert_fusion
  29.5 0.1 broadcast_in_dim.4
  29.6 24.2 %all_to_all.16 = bf16[64,2,768]{2,1,0:T(2,128)(2,1)S(1)} all-to-all(bf16[64,2,768]{2,1,0:T(2,128)(2,1)S(1)} %broadcast_in_dim.4), channel_id=1, replica_groups=mesh['z_hi'=4,'core'=2,'z_lo'=2,'x'=4,'y'=8] {'z_hi','z_lo','y'}, dimensions={0} | all-to-all | bytes 393216 | tf_op jit(solution)/shard_map/all_to_all | solution.py:153
  53.9 0.1 reshape.57.own
  53.9 0.0 copy-start
  53.9 0.0 copy-start.1
  54.0 0.0 copy-start.4
  54.0 0.1 broadcast_in_dim.5
  54.0 11.8 %all_to_all.17.rows = bf16[4,128,768]{2,1,0:T(8,128)(2,1)S(1)} all-to-all(bf16[4,128,768]{2,1,0:T(8,128)(2,1)S(1)} %broadcast_in_dim.5), channel_id=1, replica_groups=mesh['z_hi'=4,'core'=2,'z_lo'=2,'x'=4,'y'=8] {'x'}, dimensions={0} | all-to-all | bytes 1572864 | tf_op jit(solution)/shard_map/all_to_all | solution.py:153
  65.8 5.9 %collective-permute-start.1 = (bf16[4,128,768]{2,1,0:T(8,128)(2,1)S(1)}, bf16[4,128,768]{2,1,0:T(8,128)(2,1)}, u32[]{:S(2)}, u32[]{:S(2)}) collective-permute-start(bf16[4,128,768]{2,1,0:T(8,128)(2,1)S(1)} %all_to_all.17.rows), channel_id=1, source_target_pairs={{0,64},{64,0},{1,65},{65,1},{2,66},{66,2},{3,67},{67,3},{4,68},{68... | collective-permute-start | bytes 2359304 | tf_op jit(solution)/shard_map/ppermute | solution.py:157
  71.7 2.1 %collective-permute-start = (bf16[128,768]{1,0:T(8,128)(2,1)S(1)}, bf16[128,768]{1,0:T(8,128)(2,1)}, u32[]{:S(2)}, u32[]{:S(2)}) collective-permute-start(bf16[128,768]{1,0:T(8,128)(2,1)S(1)} %reshape.57.own), channel_id=1, source_target_pairs={{0,64},{64,0},{1,65},{65,1},{2,66},{66,2},{3,67},{67,3},{4,68},{68... | collective-permute-start | bytes 589832 | tf_op jit(solution)/shard_map/ppermute | solution.py:157
  73.8 1.4 %collective-permute-done.other = bf16[128,768]{1,0:T(8,128)(2,1)} collective-permute-done((bf16[128,768]{1,0:T(8,128)(2,1)S(1)}, bf16[128,768]{1,0:T(8,128)(2,1)}, u32[]{:S(2)}, u32[]{:S(2)}) %collective-permute-start) | collective-permute-done | bytes 196640 | tf_op jit(solution)/shard_map/ppermute | solution.py:157
  75.2 0.0 copy-done
  75.2 0.0 copy-done.1
  75.2 0.0 copy-done.4
  75.2 0.0 copy-start.6
  75.2 0.8 copy-done.6
  76.0 4.3 %attend_first.1 = (bf16[256,768]{1,0:T(8,128)(2,1)S(1)}, f32[256,128]{1,0:T(8,128)S(1)}, f32[256,768]{1,0:T(8,128)S(1)}) custom-call(bf16[256,128]{1,0:T(8,128)(2,1)S(1)} %copy-done.6, bf16[128,768]{1,0:T(8,128)(2,1)S(1)} %copy-done.4, bf16[128,768]{1,0:T(8,128)(2,1)S(1)} %reshape.57.own, bf16[128,768]{1,0:T(8,128)(2,1)} %collective-permute-done.other, ...), custom_call_target="tpu_custom_call" | custom-call | flops 1409286144 | bytes 1048576 | tf_op jit(solution)/shard_map/attend_first/pallas_call | solution.py:170
  80.3 0.0 copy-start.5
  80.3 9.8 %attend_next.1 = (f32[256,128]{1,0:T(8,128)S(1)}, f32[256,768]{1,0:T(8,128)S(1)}) custom-call(s32[1]{0:T(128)} %bitcast.place, bf16[256,768]{1,0:T(8,128)(2,1)S(1)} %get-tuple-element.10.q, bf16[4,128,768]{2,1,0:T(8,128)(2,1)S(1)} %all_to_all.17.rows, bf16[768,768]{1,0:T(8,128)(2,1)S(1)} %copy-done, bf16[768,768]{1,0:T(8,128)(2,1)S(1)} %copy-done.1, ...), custom_call_target="tpu_custom_call" | custom-call | flops 2113929216 | bytes 1048576 | tf_op jit(solution)/shard_map/attend_next/pallas_call | solution.py:181
  90.1 0.0 collective-permute-done.1.rows
  90.2 0.0 copy-done.5
  90.2 10.7 %attend_last.1 = bf16[256,128]{1,0:T(8,128)(2,1)} custom-call(s32[1]{0:T(128)} %bitcast.place, bf16[256,768]{1,0:T(8,128)(2,1)S(1)} %get-tuple-element.10.q, bf16[4,128,768]{2,1,0:T(8,128)(2,1)} %collective-permute-done.1.rows, bf16[768,768]{1,0:T(8,128)(2,1)S(1)} %copy-done, bf16[768,768]{1,0:T(8,128)(2,1)S(1)} %copy-done.1, ...), custom_call_target="tpu_custom_call" | custom-call | flops 2113929216 | bytes 1048576 | tf_op jit(solution)/shard_map/attend_last/pallas_call | solution.py:190
  (2 shorter events, 0.0 us)
Async XLA Ops:
  0.0 0.9 copy-start.2
  0.9 0.9 copy-start.3
  1.9 0.7 copy-start.7
  2.5 0.7 copy-start.8
  53.9 21.3 %copy-start = (bf16[768,768]{1,0:T(8,128)(2,1)S(1)}, bf16[768,768]{1,0:T(8,128)(2,1)}, u32[]{:S(2)}) copy-start(bf16[768,768]{1,0:T(8,128)(2,1)} %w_key.5) | copy-start | bytes 3538948
  53.9 21.2 %copy-start.1 = (bf16[768,768]{1,0:T(8,128)(2,1)S(1)}, bf16[768,768]{1,0:T(8,128)(2,1)}, u32[]{:S(2)}) copy-start(bf16[768,768]{1,0:T(8,128)(2,1)} %w_value.5) | copy-start | bytes 3538948
  54.0 21.2 %copy-start.4 = (bf16[128,768]{1,0:T(8,128)(2,1)S(1)}, bf16[128,768]{1,0:T(8,128)(2,1)}, u32[]{:S(2)}) copy-start(bf16[128,768]{1,0:T(8,128)(2,1)} %w_query.1) | copy-start | bytes 589828
  65.8 24.3 %collective-permute-start.1 = (bf16[4,128,768]{2,1,0:T(8,128)(2,1)S(1)}, bf16[4,128,768]{2,1,0:T(8,128)(2,1)}, u32[]{:S(2)}, u32[]{:S(2)}) collective-permute-start(bf16[4,128,768]{2,1,0:T(8,128)(2,1)S(1)} %all_to_all.17.rows), channel_id=1, source_target_pairs={{0,64},{64,0},{1,65},{65,1},{2,66},{66,2},{3,67},{67,3},{4,68},{68... | collective-permute-start | bytes 2359304 | tf_op jit(solution)/shard_map/ppermute | solution.py:157
  71.7 3.5 %collective-permute-start = (bf16[128,768]{1,0:T(8,128)(2,1)S(1)}, bf16[128,768]{1,0:T(8,128)(2,1)}, u32[]{:S(2)}, u32[]{:S(2)}) collective-permute-start(bf16[128,768]{1,0:T(8,128)(2,1)S(1)} %reshape.57.own), channel_id=1, source_target_pairs={{0,64},{64,0},{1,65},{65,1},{2,66},{66,2},{3,67},{67,3},{4,68},{68... | collective-permute-start | bytes 589832 | tf_op jit(solution)/shard_map/ppermute | solution.py:157
  75.2 0.8 copy-start.6
  80.3 9.9 %copy-start.5 = (bf16[768,128]{1,0:T(8,128)(2,1)S(1)}, bf16[768,128]{1,0:T(8,128)(2,1)}, u32[]{:S(2)}) copy-start(bf16[768,128]{1,0:T(8,128)(2,1)} %w_out.1) | copy-start | bytes 589828

commit v3 on v1

v3 whole, which is shorter than its diff:
```python
import jax
import jax.numpy as jnp
from jax import lax
from jax.experimental import pallas as pl
from jax.experimental.pallas import tpu as pltpu
from jax.sharding import Mesh
from jax.sharding import PartitionSpec as P

HEADS = 12
HEAD_DIM = 64
S_DEV = 2
AXES = ("z_hi", "core", "z_lo", "x", "y")
SHARD = ("z_lo", "x", "y")
BF16 = jnp.bfloat16
F32 = jnp.float32
PAIR = 2 * HEAD_DIM
GROUP = 4 * HEAD_DIM
VMEM = pl.BlockSpec(memory_space=pltpu.VMEM)
NN, NT, TN = ((1,), (0,)), ((1,), (1,)), ((0,), (0,))


def layer_norm(pooled):
    mean = jnp.mean(pooled, axis=-1, keepdims=True)
    centred = pooled - mean
    spread = jnp.mean(centred * centred, axis=-1, keepdims=True)
    return (centred * lax.rsqrt(spread + 1e-05)).astype(BF16)


def matmul(a, b, dims=NN):
    return lax.dot_general(a, b, (dims, ((), ())), preferred_element_type=F32)


def attend(queries, w_query, rows, w_key, w_value, store):
    q_cols, keys, values, scores, weights = {}, {}, {}, {}, {}

    def project(g):
        cols = slice(g * GROUP, (g + 1) * GROUP)
        q = matmul(w_query[:, cols].T, queries[...], NT).astype(BF16)
        q_cols[g] = q * jnp.asarray(HEAD_DIM**-0.5, BF16)
        keys[g] = matmul(rows[...], w_key[:, cols]).astype(BF16)
        values[g] = matmul(rows[...], w_value[:, cols]).astype(BF16).T

    def score(head):
        g, h = head // 4, head % 4
        q = q_cols[g][h * HEAD_DIM : (h + 1) * HEAD_DIM]
        q = jnp.concatenate([q, jnp.zeros_like(q)] if h % 2 == 0 else [jnp.zeros_like(q), q], axis=0)
        scores[head] = matmul(keys[g][:, h // 2 * PAIR : (h // 2 + 1) * PAIR], q)

    def weigh(head):
        s = scores.pop(head)
        peak = jnp.max(s, axis=0, keepdims=True)
        expo = jnp.exp(s - peak)
        weights[head] = peak, jnp.sum(expo, axis=0, keepdims=True), expo.astype(BF16)

    def finish(head):
        peak, total, expo = weights.pop(head)
        mine = slice(head % 4 * HEAD_DIM, (head % 4 + 1) * HEAD_DIM)
        store(head, peak, total, matmul(values[head // 4][mine], expo))

    lead, tail, ahead = 2, 4, 2
    project(0)
    for step in range(HEADS + tail):
        if (step + ahead) % 4 == 0 and 0 < (step + ahead) // 4 < HEADS // 4:
            project((step + ahead) // 4)
        if step < HEADS:
            score(step)
        if lead <= step < HEADS + lead:
            weigh(step - lead)
        if step >= tail:
            finish(step - tail)


def near_kernel(queries, w_query, rows, w_key, w_value, stats, summed):
    def store(head, peak, total, result):
        stats[head : head + 1, :] = peak
        stats[16 + head : 17 + head, :] = total
        summed[head * HEAD_DIM : (head + 1) * HEAD_DIM, :] = result

    attend(queries, w_query, rows, w_key, w_value, store)


def far_kernel(queries, w_query, rows, w_key, w_value, stats, summed, w_out, out, heads):
    def store(head, peak, total, result):
        mine = slice(head * HEAD_DIM, (head + 1) * HEAD_DIM)
        before = stats[head : head + 1, :]
        top = jnp.maximum(before, peak)
        old, new = jnp.exp(before - top), jnp.exp(peak - top)
        whole = stats[16 + head : 17 + head, :] * old + total * new
        heads[mine, :] = ((summed[mine, :] * old + result * new) / whole).astype(BF16)

    attend(queries, w_query, rows, w_key, w_value, store)
    out[...] = matmul(heads[...], w_out[...], TN).astype(BF16)


def attention(queries, near, w_query, w_key, w_value, w_out):
    count, width = queries.shape[0], w_query.shape[1]
    anchors = near.shape[0]
    how = dict(
        compiler_params=pltpu.CompilerParams(vmem_limit_bytes=16 * 1024 * 1024),
        cost_estimate=pl.CostEstimate(
            flops=anchors * width * (width * 4 + count * 16),
            bytes_accessed=2**20,
            transcendentals=count * anchors * HEADS,
        ),
    )
    far = lax.ppermute(near, "core", [(0, 1), (1, 0)])
    stats, summed = pl.pallas_call(
        near_kernel,
        out_shape=[jax.ShapeDtypeStruct((32, count), F32), jax.ShapeDtypeStruct((width, count), F32)],
        in_specs=[VMEM] * 5,
        out_specs=[VMEM] * 2,
        name="near",
        **how,
    )(queries, w_query, near, w_key, w_value)
    return pl.pallas_call(
        far_kernel,
        out_shape=jax.ShapeDtypeStruct((count, w_out.shape[1]), BF16),
        in_specs=[VMEM] * 8,
        out_specs=VMEM,
        scratch_shapes=[pltpu.VMEM((width, count), BF16)],
        name="far",
        **how,
    )(queries, w_query, far, w_key, w_value, stats, summed, w_out)


def spread(rows, axes):
    count = lax.axis_size(axes)
    copies = jnp.broadcast_to(rows[None], (count, *rows.shape))
    return lax.all_to_all(copies, axes, 0, 0, tiled=True).reshape(-1, rows.shape[-1])


def body(points, block_owner, block_node, queries, w_in, w_key, w_value, w_query, w_out):
    shards = lax.axis_size(SHARD)
    _, block_points, in_features = points.shape
    width = w_in.shape[1]
    node = block_owner[:, 0] * S_DEV + block_node
    messages = jax.nn.gelu(
        jnp.dot(points.reshape(-1, in_features), w_in, preferred_element_type=F32)
    ).astype(BF16)
    pick = jnp.repeat(node, block_points)[None, :] == jnp.arange(shards * S_DEV, dtype=jnp.int32)[:, None]
    partial = jnp.dot(pick.astype(BF16), messages, preferred_element_type=F32).astype(BF16)
    arrived = lax.all_to_all(partial.reshape(shards, S_DEV, width), SHARD, 0, 0, tiled=True)
    normed = layer_norm(jnp.sum(arrived.astype(F32), axis=0))
    column = spread(normed, ("z_hi", "z_lo", "y"))
    near = spread(column, ("x",))
    return attention(queries, near, w_query, w_key, w_value, w_out)


def solution(mesh):
    sizes = (mesh.shape["region"] // 2, 2, 2, 4, mesh.shape["shard"] // 8)
    fine = Mesh(mesh.devices.reshape(sizes), AXES)
    rows = P(AXES)
    return jax.shard_map(
        body,
        mesh=fine,
        in_specs=(rows, rows, rows, rows, P(), P(), P(), P(), P()),
        out_specs=rows,
        check_vma=False,
    )
```

time: 79.8 us -> 77.6 us (0.972)
  waiting for transfers between devices: 1.89 us -> 0.01 us
    ppermute x1, waiting for transfers between devices: 1.89 us -> 0.01 us  [attention(): far = lax.ppermute(near, 'core', [(0, 1), (1, 0)])]
    pallas_call x1 -> x2, Pallas kernels: 8.08 us -> 7.52 us  [the longest x1 4.18 us: attention(): pl.pallas_call(far_kernel, out_shape=jax.ShapeDtypeStruct((count, w_out.s...]
  transfers between devices with their start and end apart: 1 -> 1, of which waited for: 1 -> 0; matrix products, arithmetic and copies ran while one was open for 0% -> 0% of each run, Pallas kernels for 0% -> 4%
where the time goes in v3:
time: 77.6 us; the launch traced here: 77.3 us
  blocking collectives  59.5 us (77%)
  Pallas kernels  7.52 us (10%)
  starting transfers between devices  5.99 us (8%)
  matrix products  2.03 us (3%)
  other arithmetic  1.52 us (2%)
    all_to_all x2, blocking collectives, spread(): lax.all_to_all(copies, axes, 0, 0, tiled=True).reshape(-1, rows.shape[-1])  36.1 us
    all_to_all x1, blocking collectives, body(): lax.all_to_all(partial.reshape(shards, S_DEV, width), SHARD, 0, 0, tiled=...  23.5 us
    ppermute x1, starting transfers between devices, attention(): far = lax.ppermute(near, 'core', [(0, 1), (1, 0)])  5.99 us
    pallas_call x1, Pallas kernels, attention(): pl.pallas_call(far_kernel, out_shape=jax.ShapeDtypeStruct((count, w_out.s...  4.18 us
    pallas_call x1, Pallas kernels, attention(): pl.pallas_call(near_kernel, out_shape=[jax.ShapeDtypeStruct((32, count),...  3.34 us
    dot_general x1, matrix products, body(): jnp.dot(pick.astype(BF16), messages, preferred_element_type=F32)  2.03 us
  transfers between devices with their start and end apart: 1, of which 0 were waited for; matrix products, arithmetic and copies ran while one was open for 0% of the time, Pallas kernels for 4%

profile of v3, /device:TPU:1, one launch (start us, length us, event | category | flops | bytes accessed | tf_op | source)
XLA Modules:
  0.0 77.3 jit_solution(12653004813720953264)
XLA Ops:
  0.0 0.0 copy-start
  0.0 0.7 bitcast_add_fusion
  0.7 0.1 broadcast_in_dim.8
  0.8 0.1 eq.15
  0.9 0.1 copy-done
  1.0 2.0 %fusion.13 = bf16[128,768]{1,0:T(8,128)(2,1)S(1)} fusion(bf16[128,768]{1,0:T(8,128)(2,1)S(1)} %copy-done, bf16[96,8,128]{2,1,0:T(8,128)(2,1)} %param.9, s32[768]{0:T(1024)S(1)} %eq.15), kind=kOutput, calls=%fused_computation.14 | convolution fusion | flops 307494912 | bytes 592896 | tf_op jit(solution)/shard_map/dot_general | solution.py:141
  3.0 0.1 reshape.55
  3.1 23.5 %all_to_all.15 = bf16[64,2,768]{2,1,0:T(2,128)(2,1)S(1)} all-to-all(bf16[64,2,768]{2,1,0:T(2,128)(2,1)S(1)} %reshape.55), channel_id=1, replica_groups=mesh['z_hi'=4,'core'=2,'z_lo'=2,'x'=4,'y'=8] {'z_lo','x','y'}, dimensions={0} | all-to-all | bytes 393216 | tf_op jit(solution)/shard_map/all_to_all | solution.py:142
  26.5 0.5 convert_reduce_fusion
  27.1 0.2 multiply_reduce_fusion
  27.3 0.1 multiply_convert_fusion
  27.4 0.1 broadcast_in_dim.9
  27.5 24.2 %all_to_all.16 = bf16[64,2,768]{2,1,0:T(2,128)(2,1)S(1)} all-to-all(bf16[64,2,768]{2,1,0:T(2,128)(2,1)S(1)} %broadcast_in_dim.9), channel_id=1, replica_groups=mesh['z_hi'=4,'core'=2,'z_lo'=2,'x'=4,'y'=8] {'z_hi','z_lo','y'}, dimensions={0} | all-to-all | bytes 393216 | tf_op jit(solution)/shard_map/all_to_all | solution.py:129
  51.7 0.0 copy-start.5
  51.7 0.1 broadcast_in_dim.10
  51.8 0.0 copy-start.1
  51.8 0.0 copy-start.2
  51.8 0.0 copy-start.3
  51.8 0.1 broadcast_in_dim.22
  51.9 11.8 %all_to_all.17 = bf16[4,128,768]{2,1,0:T(8,128)(2,1)S(1)} all-to-all(bf16[4,128,768]{2,1,0:T(8,128)(2,1)S(1)} %broadcast_in_dim.22), channel_id=1, replica_groups=mesh['z_hi'=4,'core'=2,'z_lo'=2,'x'=4,'y'=8] {'x'}, dimensions={0} | all-to-all | bytes 1572864 | tf_op jit(solution)/shard_map/all_to_all | solution.py:129
  63.7 0.0 copy-start.4
  63.7 6.0 %collective-permute-start = (bf16[512,768]{1,0:T(8,128)(2,1)S(1)}, bf16[512,768]{1,0:T(8,128)(2,1)S(1)}, u32[]{:S(2)}, u32[]{:S(2)}) collective-permute-start(bf16[512,768]{1,0:T(8,128)(2,1)S(1)} %bitcast.8), channel_id=1, source_target_pairs={{0,64},{64,0},{1,65},{65,1},{2,66},{66,2},{3,67},{67,3},{4,68},{68... | collective-permute-start | bytes 2359304 | tf_op jit(solution)/shard_map/ppermute | solution.py:106
  69.7 0.0 copy-done.5
  69.7 0.0 copy-done.1
  69.7 0.0 copy-done.2
  69.7 0.0 copy-done.3
  69.8 3.3 %near.1 = (f32[32,256]{1,0:T(8,128)S(1)}, f32[768,256]{1,0:T(8,128)S(1)}) custom-call(bf16[256,128]{1,0:T(8,128)(2,1)S(1)} %copy-done.5, bf16[128,768]{1,0:T(8,128)(2,1)S(1)} %copy-done.3, bf16[512,768]{1,0:T(8,128)(2,1)S(1)} %bitcast.9, bf16[768,768]{1,0:T(8,128)(2,1)S(1)} %copy-done.1, bf16[768,768]{1,0:T(8,128)(2,1)S(1)} %copy-done.2), custom_call_target="tpu_custom_call" | custom-call | flops 2818572288 | bytes 1048576 | tf_op jit(solution)/shard_map/near/pallas_call | solution.py:107
  73.1 0.0 collective-permute-done.rows
  73.1 0.0 copy-done.4
  73.1 4.2 %far.1 = bf16[256,128]{1,0:T(8,128)(2,1)} custom-call(bf16[256,128]{1,0:T(8,128)(2,1)S(1)} %copy-done.5, bf16[128,768]{1,0:T(8,128)(2,1)S(1)} %copy-done.3, bf16[512,768]{1,0:T(8,128)(2,1)S(1)} %collective-permute-done.rows, bf16[768,768]{1,0:T(8,128)(2,1)S(1)} %copy-done.1, bf16[768,768]{1,0:T(8,128)(2,1)S(1)} %copy-done.2, ...), custom_call_target="tpu_custom_call" | custom-call | flops 2818572288 | bytes 1048576 | tf_op jit(solution)/shard_map/far/pallas_call | solution.py:115
  (2 shorter events, 0.0 us)
Async XLA Ops:
  0.0 1.0 %copy-start = (bf16[128,768]{1,0:T(8,128)(2,1)S(1)}, bf16[128,768]{1,0:T(8,128)(2,1)}, u32[]{:S(2)}) copy-start(bf16[128,768]{1,0:T(8,128)(2,1)} %param.13) | copy-start | bytes 589828
  51.7 18.0 %copy-start.5 = (bf16[256,128]{1,0:T(8,128)(2,1)S(1)}, bf16[256,128]{1,0:T(8,128)(2,1)}, u32[]{:S(2)}) copy-start(bf16[256,128]{1,0:T(8,128)(2,1)} %queries.3) | copy-start | bytes 196612
  51.8 17.9 %copy-start.1 = (bf16[768,768]{1,0:T(8,128)(2,1)S(1)}, bf16[768,768]{1,0:T(8,128)(2,1)}, u32[]{:S(2)}) copy-start(bf16[768,768]{1,0:T(8,128)(2,1)} %w_key.3) | copy-start | bytes 3538948
  51.8 17.9 %copy-start.2 = (bf16[768,768]{1,0:T(8,128)(2,1)S(1)}, bf16[768,768]{1,0:T(8,128)(2,1)}, u32[]{:S(2)}) copy-start(bf16[768,768]{1,0:T(8,128)(2,1)} %w_value.3) | copy-start | bytes 3538948
  51.8 17.9 %copy-start.3 = (bf16[128,768]{1,0:T(8,128)(2,1)S(1)}, bf16[128,768]{1,0:T(8,128)(2,1)}, u32[]{:S(2)}) copy-start(bf16[128,768]{1,0:T(8,128)(2,1)} %w_query.3) | copy-start | bytes 589828
  63.7 9.4 %copy-start.4 = (bf16[768,128]{1,0:T(8,128)(2,1)S(1)}, bf16[768,128]{1,0:T(8,128)(2,1)}, u32[]{:S(2)}) copy-start(bf16[768,128]{1,0:T(8,128)(2,1)} %w_out.1) | copy-start | bytes 589828
  63.7 9.4 %collective-permute-start = (bf16[512,768]{1,0:T(8,128)(2,1)S(1)}, bf16[512,768]{1,0:T(8,128)(2,1)S(1)}, u32[]{:S(2)}, u32[]{:S(2)}) collective-permute-start(bf16[512,768]{1,0:T(8,128)(2,1)S(1)} %bitcast.8), channel_id=1, source_target_pairs={{0,64},{64,0},{1,65},{65,1},{2,66},{66,2},{3,67},{67,3},{4,68},{68... | collective-permute-start | bytes 2359304 | tf_op jit(solution)/shard_map/ppermute | solution.py:106

commit v4 on v3

--- a/solution.py
+++ b/solution.py
@@ -1,3 +1,6 @@
+import functools
+import math
+
 import jax
 import jax.numpy as jnp
 from jax import lax
@@ -9,6 +12,8 @@
 HEADS = 12
 HEAD_DIM = 64
 S_DEV = 2
+GELU_A = 2 * (2 / math.pi) ** 0.5
+GELU_B = 4 * 0.044715 * GELU_A
 AXES = ("z_hi", "core", "z_lo", "x", "y")
 SHARD = ("z_lo", "x", "y")
 BF16 = jnp.bfloat16
@@ -16,6 +21,7 @@
 PAIR = 2 * HEAD_DIM
 GROUP = 4 * HEAD_DIM
 VMEM = pl.BlockSpec(memory_space=pltpu.VMEM)
+HBM = pl.BlockSpec(memory_space=pltpu.HBM)
 NN, NT, TN = ((1,), (0,)), ((1,), (1,)), ((0,), (0,))
 
 
@@ -30,7 +36,66 @@
     return lax.dot_general(a, b, (dims, ((), ())), preferred_element_type=F32)
 
 
-def attend(queries, w_query, rows, w_key, w_value, store):
+def pool_kernel(block_points, owner_in, node_in, points_in, w_in_in, out, owner, node, points, w_in, pick, sems):
+    pairs = ((owner_in, owner), (node_in, node), (w_in_in, w_in), (points_in, points))
+    copies = [pltpu.make_async_copy(a, b, sems.at[i]) for i, (a, b) in enumerate(pairs)]
+    for copy in copies:
+        copy.start()
+    blocks, slots = owner.shape[0], pick.shape[1]
+    rows = 2 * block_points
+    lane = lax.broadcasted_iota(jnp.int32, (rows, slots), 1)
+    first = lax.broadcasted_iota(jnp.int32, (rows, slots), 0) < block_points
+    copies[0].wait()
+    copies[1].wait()
+    for pair in range(blocks // 2):
+        ids = [owner[b] * S_DEV + node[b] for b in (2 * pair, 2 * pair + 1)]
+        chosen = lane == jnp.where(first, ids[0], ids[1])
+        pick[rows * pair : rows * (pair + 1), :] = jnp.where(chosen, 1.0, 0.0).astype(BF16)
+    copies[2].wait()
+    copies[3].wait()
+    messages = {}
+    groups = w_in.shape[1] // GROUP
+
+    def send(g):
+        half = matmul(points[...], w_in[:, g * GROUP : (g + 1) * GROUP]) * 0.5
+        inner = half * (GELU_A + GELU_B * (half * half))
+        messages[g] = (half + half * jnp.tanh(inner)).astype(BF16)
+
+    def gather(g):
+        pooled = matmul(pick[...], messages.pop(g), TN).astype(BF16)
+        cols = slice(g * GROUP, (g + 1) * GROUP)
+        out[:, :, cols] = pooled.reshape(out.shape[0], out.shape[1], GROUP)
+
+    for g in range(groups + 1):
+        if g < groups:
+            send(g)
+        if g > 0:
+            gather(g - 1)
+
+
+def pool(points, owner, node, w_in, slots):
+    blocks, block_points, features = points.shape
+    rows = blocks * block_points
+    return pl.pallas_call(
+        functools.partial(pool_kernel, block_points),
+        out_shape=jax.ShapeDtypeStruct((slots // S_DEV, S_DEV, w_in.shape[1]), BF16),
+        in_specs=[HBM] * 4,
+        out_specs=VMEM,
+        scratch_shapes=[
+            pltpu.SMEM((blocks,), jnp.int32),
+            pltpu.SMEM((blocks,), jnp.int32),
+            pltpu.VMEM((rows, features), BF16),
+            pltpu.VMEM(w_in.shape, BF16),
+            pltpu.VMEM((rows, slots), BF16),
+            pltpu.SemaphoreType.DMA((4,)),
+        ],
+        compiler_params=pltpu.CompilerParams(vmem_limit_bytes=60 * 1024 * 1024),
+        cost_estimate=pl.CostEstimate(flops=2**28, bytes_accessed=2**20, transcendentals=2**19),
+        name="pool",
+    )(owner, node, points.reshape(rows, features), w_in)
+
+
+def attend(queries, w_query, rows, w_key, w_value, store, tail, ahead):
     q_cols, keys, values, scores, weights = {}, {}, {}, {}, {}
 
     def project(g):
@@ -57,7 +122,7 @@
         mine = slice(head % 4 * HEAD_DIM, (head % 4 + 1) * HEAD_DIM)
         store(head, peak, total, matmul(values[head // 4][mine], expo))
 
-    lead, tail, ahead = 2, 4, 2
+    lead = tail - 2
     project(0)
     for step in range(HEADS + tail):
         if (step + ahead) % 4 == 0 and 0 < (step + ahead) // 4 < HEADS // 4:
@@ -76,7 +141,7 @@
         stats[16 + head : 17 + head, :] = total
         summed[head * HEAD_DIM : (head + 1) * HEAD_DIM, :] = result
 
-    attend(queries, w_query, rows, w_key, w_value, store)
+    attend(queries, w_query, rows, w_key, w_value, store, 4, 3)
 
 
 def far_kernel(queries, w_query, rows, w_key, w_value, stats, summed, w_out, out, heads):
@@ -85,10 +150,10 @@
         before = stats[head : head + 1, :]
         top = jnp.maximum(before, peak)
         old, new = jnp.exp(before - top), jnp.exp(peak - top)
-        whole = stats[16 + head : 17 + head, :] * old + total * new
-        heads[mine, :] = ((summed[mine, :] * old + result * new) / whole).astype(BF16)
-
-    attend(queries, w_query, rows, w_key, w_value, store)
+        share = 1.0 / (stats[16 + head : 17 + head, :] * old + total * new)
+        heads[mine, :] = (summed[mine, :] * (old * share) + result * (new * share)).astype(BF16)
+
+    attend(queries, w_query, rows, w_key, w_value, store, 5, 2)
     out[...] = matmul(heads[...], w_out[...], TN).astype(BF16)
 
 
@@ -123,6 +188,22 @@
     )(queries, w_query, far, w_key, w_value, stats, summed, w_out)
 
 
+def norm_kernel(arrived, out):
+    normed = layer_norm(jnp.sum(arrived[...].astype(F32), axis=0))
+    out[...] = jnp.broadcast_to(normed[None], out.shape)
+
+
+def normed_copies(arrived, axes):
+    return pl.pallas_call(
+        norm_kernel,
+        out_shape=jax.ShapeDtypeStruct((lax.axis_size(axes), *arrived.shape[1:]), BF16),
+        in_specs=[VMEM],
+        out_specs=VMEM,
+        compiler_params=pltpu.CompilerParams(vmem_limit_bytes=16 * 1024 * 1024),
+        name="norm",
+    )(arrived)
+
+
 def spread(rows, axes):
     count = lax.axis_size(axes)
     copies = jnp.broadcast_to(rows[None], (count, *rows.shape))
@@ -131,17 +212,11 @@
 
 def body(points, block_owner, block_node, queries, w_in, w_key, w_value, w_query, w_out):
     shards = lax.axis_size(SHARD)
-    _, block_points, in_features = points.shape
     width = w_in.shape[1]
-    node = block_owner[:, 0] * S_DEV + block_node
-    messages = jax.nn.gelu(
-        jnp.dot(points.reshape(-1, in_features), w_in, preferred_element_type=F32)
-    ).astype(BF16)
-    pick = jnp.repeat(node, block_points)[None, :] == jnp.arange(shards * S_DEV, dtype=jnp.int32)[:, None]
-    partial = jnp.dot(pick.astype(BF16), messages, preferred_element_type=F32).astype(BF16)
+    partial = pool(points, block_owner[:, 0], block_node, w_in, shards * S_DEV)
     arrived = lax.all_to_all(partial.reshape(shards, S_DEV, width), SHARD, 0, 0, tiled=True)
-    normed = layer_norm(jnp.sum(arrived.astype(F32), axis=0))
-    column = spread(normed, ("z_hi", "z_lo", "y"))
+    copies = normed_copies(arrived, ("z_hi", "z_lo", "y"))
+    column = lax.all_to_all(copies, ("z_hi", "z_lo", "y"), 0, 0, tiled=True).reshape(-1, width)
     near = spread(column, ("x",))
     return attention(queries, near, w_query, w_key, w_value, w_out)
 

time: 77.6 us -> 77 us (level)
  Pallas kernels: 7.52 us -> 10.8 us
  matrix products: 2.03 us -> 0 us
  other arithmetic: 1.52 us -> 0 us
    all_to_all x0 -> x1, blocking collectives: none -> 24.2 us  [body(): lax.all_to_all(copies, ('z_hi', 'z_lo', 'y'), 0, 0, tiled=True)]
    all_to_all x2 -> x1, blocking collectives: 36.1 us -> 11.8 us  [spread(): lax.all_to_all(copies, axes, 0, 0, tiled=True).reshape(-1, rows.shape[-1])]
    pallas_call x0 -> x2, Pallas kernels: none -> 3.32 us  [the longest x1 2.94 us: pool(): pl.pallas_call(functools.partial(pool_kernel, block_points), out_shape=ja...]
    dot_general x1 -> x0, matrix products: 2.03 us -> none  [body(): jnp.dot(pick.astype(BF16), messages, preferred_element_type=F32)]
where the time goes in v4:
time: 77 us; the launch traced here: 76.7 us
  blocking collectives  59.7 us (78%)
  Pallas kernels  10.8 us (14%)
  starting transfers between devices  5.99 us (8%)
    all_to_all x1, blocking collectives, body(): lax.all_to_all(copies, ('z_hi', 'z_lo', 'y'), 0, 0, tiled=True)  24.2 us
    all_to_all x1, blocking collectives, body(): lax.all_to_all(partial.reshape(shards, S_DEV, width), SHARD, 0, 0, tiled=...  23.7 us
    all_to_all x1, blocking collectives, spread(): lax.all_to_all(copies, axes, 0, 0, tiled=True).reshape(-1, rows.shape[-1])  11.8 us
    ppermute x1, starting transfers between devices, attention(): far = lax.ppermute(near, 'core', [(0, 1), (1, 0)])  5.99 us
    pallas_call x1, Pallas kernels, attention(): pl.pallas_call(far_kernel, out_shape=jax.ShapeDtypeStruct((count, w_out.s...  4.1 us
    pallas_call x1, Pallas kernels, attention(): pl.pallas_call(near_kernel, out_shape=[jax.ShapeDtypeStruct((32, count),...  3.33 us
    pallas_call x1, Pallas kernels, pool(): pl.pallas_call(functools.partial(pool_kernel, block_points), out_shape=ja...  2.94 us
  transfers between devices with their start and end apart: 1, of which 0 were waited for; matrix products, arithmetic and copies ran while one was open for 0% of the time, Pallas kernels for 4%

profile of v4, /device:TPU:1, one launch (start us, length us, event | category | flops | bytes accessed | tf_op | source)
XLA Modules:
  0.0 76.7 jit_solution(10748870852099712569)
XLA Ops:
  0.0 2.9 %pool.1 = bf16[64,2,768]{2,1,0:T(2,128)(2,1)} custom-call(s32[96]{0:T(128)} %bitcast.6, s32[96]{0:T(128)} %node_in.1, bf16[768,128]{1,0:T(8,128)(2,1)} %bitcast.5, bf16[128,768]{1,0:T(8,128)(2,1)} %w_in_in.1), custom_call_target="tpu_custom_call" | custom-call | flops 268435456 | bytes 1048576 | tf_op jit(solution)/shard_map/pool/pallas_call | solution.py:79
  2.9 23.7 %all_to_all.15.arrived = bf16[64,2,768]{2,1,0:T(2,128)(2,1)S(1)} all-to-all(bf16[64,2,768]{2,1,0:T(2,128)(2,1)} %pool.1), channel_id=1, replica_groups=mesh['z_hi'=4,'core'=2,'z_lo'=2,'x'=4,'y'=8] {'z_lo','x','y'}, dimensions={0} | all-to-all | bytes 393216 | tf_op jit(solution)/shard_map/all_to_all | solution.py:217
  26.6 0.4 norm.1
  27.0 24.2 %all_to_all.16 = bf16[64,2,768]{2,1,0:T(2,128)(2,1)S(1)} all-to-all(bf16[64,2,768]{2,1,0:T(2,128)(2,1)S(1)} %norm.1), channel_id=1, replica_groups=mesh['z_hi'=4,'core'=2,'z_lo'=2,'x'=4,'y'=8] {'z_hi','z_lo','y'}, dimensions={0} | all-to-all | bytes 393216 | tf_op jit(solution)/shard_map/all_to_all | solution.py:219
  51.2 0.0 copy-start.4
  51.2 0.1 broadcast_in_dim.7
  51.3 0.0 copy-start
  51.3 0.0 copy-start.1
  51.3 0.0 copy-start.2
  51.4 0.1 broadcast_in_dim.8
  51.4 11.8 %all_to_all.17 = bf16[4,128,768]{2,1,0:T(8,128)(2,1)S(1)} all-to-all(bf16[4,128,768]{2,1,0:T(8,128)(2,1)S(1)} %broadcast_in_dim.8), channel_id=1, replica_groups=mesh['z_hi'=4,'core'=2,'z_lo'=2,'x'=4,'y'=8] {'x'}, dimensions={0} | all-to-all | bytes 1572864 | tf_op jit(solution)/shard_map/all_to_all | solution.py:210
  63.2 0.0 copy-start.3
  63.2 6.0 %collective-permute-start = (bf16[512,768]{1,0:T(8,128)(2,1)S(1)}, bf16[512,768]{1,0:T(8,128)(2,1)S(1)}, u32[]{:S(2)}, u32[]{:S(2)}) collective-permute-start(bf16[512,768]{1,0:T(8,128)(2,1)S(1)} %bitcast.3), channel_id=1, source_target_pairs={{0,64},{64,0},{1,65},{65,1},{2,66},{66,2},{3,67},{67,3},{4,68},{68... | collective-permute-start | bytes 2359304 | tf_op jit(solution)/shard_map/ppermute | solution.py:171
  69.2 0.0 copy-done.4
  69.2 0.0 copy-done
  69.3 0.0 copy-done.1
  69.3 0.0 copy-done.2
  69.3 3.3 %near.1 = (f32[32,256]{1,0:T(8,128)S(1)}, f32[768,256]{1,0:T(8,128)S(1)}) custom-call(bf16[256,128]{1,0:T(8,128)(2,1)S(1)} %copy-done.4, bf16[128,768]{1,0:T(8,128)(2,1)S(1)} %copy-done.2, bf16[512,768]{1,0:T(8,128)(2,1)S(1)} %bitcast.4, bf16[768,768]{1,0:T(8,128)(2,1)S(1)} %copy-done, bf16[768,768]{1,0:T(8,128)(2,1)S(1)} %copy-done.1), custom_call_target="tpu_custom_call" | custom-call | flops 2818572288 | bytes 1048576 | tf_op jit(solution)/shard_map/near/pallas_call | solution.py:172
  72.6 0.0 collective-permute-done.rows
  72.6 0.0 copy-done.3
  72.6 4.1 %far.1 = bf16[256,128]{1,0:T(8,128)(2,1)} custom-call(bf16[256,128]{1,0:T(8,128)(2,1)S(1)} %copy-done.4, bf16[128,768]{1,0:T(8,128)(2,1)S(1)} %copy-done.2, bf16[512,768]{1,0:T(8,128)(2,1)S(1)} %collective-permute-done.rows, bf16[768,768]{1,0:T(8,128)(2,1)S(1)} %copy-done, bf16[768,768]{1,0:T(8,128)(2,1)S(1)} %copy-done.1, ...), custom_call_target="tpu_custom_call" | custom-call | flops 2818572288 | bytes 1048576 | tf_op jit(solution)/shard_map/far/pallas_call | solution.py:180
Async XLA Ops:
  51.2 18.0 %copy-start.4 = (bf16[256,128]{1,0:T(8,128)(2,1)S(1)}, bf16[256,128]{1,0:T(8,128)(2,1)}, u32[]{:S(2)}) copy-start(bf16[256,128]{1,0:T(8,128)(2,1)} %queries.3) | copy-start | bytes 196612
  51.3 17.9 %copy-start = (bf16[768,768]{1,0:T(8,128)(2,1)S(1)}, bf16[768,768]{1,0:T(8,128)(2,1)}, u32[]{:S(2)}) copy-start(bf16[768,768]{1,0:T(8,128)(2,1)} %w_key.3) | copy-start | bytes 3538948
  51.3 17.9 %copy-start.1 = (bf16[768,768]{1,0:T(8,128)(2,1)S(1)}, bf16[768,768]{1,0:T(8,128)(2,1)}, u32[]{:S(2)}) copy-start(bf16[768,768]{1,0:T(8,128)(2,1)} %w_value.3) | copy-start | bytes 3538948
  51.3 17.9 %copy-start.2 = (bf16[128,768]{1,0:T(8,128)(2,1)S(1)}, bf16[128,768]{1,0:T(8,128)(2,1)}, u32[]{:S(2)}) copy-start(bf16[128,768]{1,0:T(8,128)(2,1)} %w_query.3) | copy-start | bytes 589828
  63.2 9.4 %copy-start.3 = (bf16[768,128]{1,0:T(8,128)(2,1)S(1)}, bf16[768,128]{1,0:T(8,128)(2,1)}, u32[]{:S(2)}) copy-start(bf16[768,128]{1,0:T(8,128)(2,1)} %w_out.1) | copy-start | bytes 589828
  63.2 9.4 %collective-permute-start = (bf16[512,768]{1,0:T(8,128)(2,1)S(1)}, bf16[512,768]{1,0:T(8,128)(2,1)S(1)}, u32[]{:S(2)}, u32[]{:S(2)}) collective-permute-start(bf16[512,768]{1,0:T(8,128)(2,1)S(1)} %bitcast.3), channel_id=1, source_target_pairs={{0,64},{64,0},{1,65},{65,1},{2,66},{66,2},{3,67},{67,3},{4,68},{68... | collective-permute-start | bytes 2359304 | tf_op jit(solution)/shard_map/ppermute | solution.py:171

commit v5 on v4

--- a/solution.py
+++ b/solution.py
@@ -52,19 +52,20 @@
         chosen = lane == jnp.where(first, ids[0], ids[1])
         pick[rows * pair : rows * (pair + 1), :] = jnp.where(chosen, 1.0, 0.0).astype(BF16)
     copies[2].wait()
+    w_in[...] = w_in[...] * jnp.asarray(0.5, BF16)
     copies[3].wait()
     messages = {}
-    groups = w_in.shape[1] // GROUP
+    groups = w_in.shape[1] // 256
 
     def send(g):
-        half = matmul(points[...], w_in[:, g * GROUP : (g + 1) * GROUP]) * 0.5
+        half = matmul(points[...], w_in[:, g * 256 : (g + 1) * 256])
         inner = half * (GELU_A + GELU_B * (half * half))
         messages[g] = (half + half * jnp.tanh(inner)).astype(BF16)
 
     def gather(g):
         pooled = matmul(pick[...], messages.pop(g), TN).astype(BF16)
-        cols = slice(g * GROUP, (g + 1) * GROUP)
-        out[:, :, cols] = pooled.reshape(out.shape[0], out.shape[1], GROUP)
+        cols = slice(g * 256, (g + 1) * 256)
+        out[:, :, cols] = pooled.reshape(out.shape[0], out.shape[1], 256)
 
     for g in range(groups + 1):
         if g < groups:
@@ -89,25 +90,23 @@
             pltpu.VMEM((rows, slots), BF16),
             pltpu.SemaphoreType.DMA((4,)),
         ],
-        compiler_params=pltpu.CompilerParams(vmem_limit_bytes=60 * 1024 * 1024),
+        compiler_params=pltpu.CompilerParams(
+            vmem_limit_bytes=60 * 1024 * 1024
+        ),
         cost_estimate=pl.CostEstimate(flops=2**28, bytes_accessed=2**20, transcendentals=2**19),
         name="pool",
     )(owner, node, points.reshape(rows, features), w_in)
 
 
-def attend(queries, w_query, rows, w_key, w_value, store, tail, ahead):
-    q_cols, keys, values, scores, weights = {}, {}, {}, {}, {}
+def attend(q_cols, keys_of, values_of, store, tail, ahead):
+    keys, values, scores, weights = {}, {}, {}, {}
 
     def project(g):
-        cols = slice(g * GROUP, (g + 1) * GROUP)
-        q = matmul(w_query[:, cols].T, queries[...], NT).astype(BF16)
-        q_cols[g] = q * jnp.asarray(HEAD_DIM**-0.5, BF16)
-        keys[g] = matmul(rows[...], w_key[:, cols]).astype(BF16)
-        values[g] = matmul(rows[...], w_value[:, cols]).astype(BF16).T
+        keys[g], values[g] = keys_of(g), values_of(g)
 
     def score(head):
         g, h = head // 4, head % 4
-        q = q_cols[g][h * HEAD_DIM : (h + 1) * HEAD_DIM]
+        q = q_cols[head * HEAD_DIM : (head + 1) * HEAD_DIM, :]
         q = jnp.concatenate([q, jnp.zeros_like(q)] if h % 2 == 0 else [jnp.zeros_like(q), q], axis=0)
         scores[head] = matmul(keys[g][:, h // 2 * PAIR : (h // 2 + 1) * PAIR], q)
 
@@ -135,57 +134,119 @@
             finish(step - tail)
 
 
-def near_kernel(queries, w_query, rows, w_key, w_value, stats, summed):
+def query_kernel(queries, other_queries, w_query, own, other):
+    turned = w_query[...].T
+    for source, target in ((queries, own), (other_queries, other)):
+        target[...] = matmul(turned, source[...], NT).astype(BF16) * jnp.asarray(HEAD_DIM**-0.5, BF16)
+
+
+def give_kernel(q_cols, rows, w_key, w_value, keys, values, given):
+    def keys_of(g):
+        cols = slice(g * GROUP, (g + 1) * GROUP)
+        part = matmul(rows[...], w_key[:, cols]).astype(BF16)
+        keys[:, cols] = part
+        return part
+
+    def values_of(g):
+        cols = slice(g * GROUP, (g + 1) * GROUP)
+        part = matmul(rows[...], w_value[:, cols]).astype(BF16).T
+        values[cols, :] = part
+        return part
+
+    width = values.shape[0]
+    gathered = []
+
+    def store(head, peak, total, result):
+        given[head * HEAD_DIM : (head + 1) * HEAD_DIM, :] = result.astype(BF16)
+        gathered.append((peak, total))
+        if head == HEADS - 1:
+            rest = jnp.concatenate([p for p, _ in gathered] + [t for _, t in gathered], axis=0)
+            for term in range(3):
+                part = rest.astype(BF16)
+                at = width + 32 * term
+                given[at : at + 2 * HEADS, :] = part
+                given[at + 2 * HEADS : at + 32, :] = jnp.zeros((32 - 2 * HEADS, part.shape[1]), BF16)
+                rest = rest - part.astype(F32)
+
+    attend(q_cols, keys_of, values_of, store, 4, 3)
+
+
+def own_kernel(q_cols, keys, values, stats, summed):
     def store(head, peak, total, result):
         stats[head : head + 1, :] = peak
-        stats[16 + head : 17 + head, :] = total
+        stats[HEADS + head : HEADS + head + 1, :] = total
         summed[head * HEAD_DIM : (head + 1) * HEAD_DIM, :] = result
 
-    attend(queries, w_query, rows, w_key, w_value, store, 4, 3)
-
-
-def far_kernel(queries, w_query, rows, w_key, w_value, stats, summed, w_out, out, heads):
-    def store(head, peak, total, result):
+    def keys_of(g):
+        return keys[:, g * GROUP : (g + 1) * GROUP]
+
+    def values_of(g):
+        return values[g * GROUP : (g + 1) * GROUP, :]
+
+    attend(q_cols, keys_of, values_of, store, 4, 3)
+
+
+def merge_kernel(stats, summed, given, w_out, out, heads):
+    width = summed.shape[0]
+    terms = [given[width + 32 * t : width + 32 * t + 2 * HEADS, :].astype(F32) for t in range(3)]
+    other = (terms[2] + terms[1]) + terms[0]
+    peaks, totals = (stats[:HEADS, :], other[:HEADS]), (stats[HEADS : 2 * HEADS, :], other[HEADS:])
+    top = jnp.maximum(*peaks)
+    old, new = jnp.exp(peaks[0] - top), jnp.exp(peaks[1] - top)
+    share = 1.0 / (totals[0] * old + totals[1] * new)
+    old, new = old * share, new * share
+    for head in range(HEADS):
         mine = slice(head * HEAD_DIM, (head + 1) * HEAD_DIM)
-        before = stats[head : head + 1, :]
-        top = jnp.maximum(before, peak)
-        old, new = jnp.exp(before - top), jnp.exp(peak - top)
-        share = 1.0 / (stats[16 + head : 17 + head, :] * old + total * new)
-        heads[mine, :] = (summed[mine, :] * (old * share) + result * (new * share)).astype(BF16)
-
-    attend(queries, w_query, rows, w_key, w_value, store, 5, 2)
+        both = summed[mine, :] * old[head : head + 1] + given[mine, :].astype(F32) * new[head : head + 1]
+        heads[mine, :] = both.astype(BF16)
     out[...] = matmul(heads[...], w_out[...], TN).astype(BF16)
 
 
-def attention(queries, near, w_query, w_key, w_value, w_out):
-    count, width = queries.shape[0], w_query.shape[1]
+def call(kernel, shapes, operands, scratch=(), flops=0, exps=0):
+    return pl.pallas_call(
+        kernel,
+        out_shape=shapes,
+        in_specs=[VMEM] * len(operands),
+        out_specs=[VMEM] * len(shapes),
+        scratch_shapes=list(scratch),
+        compiler_params=pltpu.CompilerParams(vmem_limit_bytes=16 * 1024 * 1024),
+        cost_estimate=pl.CostEstimate(flops=flops, bytes_accessed=2**20, transcendentals=exps),
+    )(*operands)
+
+
+def swap(rows):
+    return lax.ppermute(rows, "core", [(0, 1), (1, 0)])
+
+
+def attention(q_own, q_other, near, w_key, w_value, w_out):
+    width, count = q_own.shape
     anchors = near.shape[0]
-    how = dict(
-        compiler_params=pltpu.CompilerParams(vmem_limit_bytes=16 * 1024 * 1024),
-        cost_estimate=pl.CostEstimate(
-            flops=anchors * width * (width * 4 + count * 16),
-            bytes_accessed=2**20,
-            transcendentals=count * anchors * HEADS,
-        ),
+    flops, exps = anchors * width * count * 16, count * anchors * HEADS
+    keys, values, given = call(
+        give_kernel,
+        [
+            jax.ShapeDtypeStruct((anchors, width), BF16),
+            jax.ShapeDtypeStruct((width, anchors), BF16),
+            jax.ShapeDtypeStruct((width + 96, count), BF16),
+        ],
+        (q_other, near, w_key, w_value),
+        flops=flops * 2,
+        exps=exps,
     )
-    far = lax.ppermute(near, "core", [(0, 1), (1, 0)])
-    stats, summed = pl.pallas_call(
-        near_kernel,
-        out_shape=[jax.ShapeDtypeStruct((32, count), F32), jax.ShapeDtypeStruct((width, count), F32)],
-        in_specs=[VMEM] * 5,
-        out_specs=[VMEM] * 2,
-        name="near",
-        **how,
-    )(queries, w_query, near, w_key, w_value)
-    return pl.pallas_call(
-        far_kernel,
-        out_shape=jax.ShapeDtypeStruct((count, w_out.shape[1]), BF16),
-        in_specs=[VMEM] * 8,
-        out_specs=VMEM,
-        scratch_shapes=[pltpu.VMEM((width, count), BF16)],
-        name="far",
-        **how,
-    )(queries, w_query, far, w_key, w_value, stats, summed, w_out)
+    given = swap(given)
+    stats, summed = call(
+        own_kernel,
+        [jax.ShapeDtypeStruct((2 * HEADS, count), F32), jax.ShapeDtypeStruct((width, count), F32)],
+        (q_own, keys, values),
+        flops=flops,
+        exps=exps,
+    )
+    return call(
+        merge_kernel,
+        [jax.ShapeDtypeStruct((count, w_out.shape[1]), BF16)],
+        (stats, summed, given, w_out),
+        scratch=[pltpu.VMEM((width, count), BF16)],
+    )[0]
 
 
 def norm_kernel(arrived, out):
@@ -215,10 +276,13 @@
     width = w_in.shape[1]
     partial = pool(points, block_owner[:, 0], block_node, w_in, shards * S_DEV)
     arrived = lax.all_to_all(partial.reshape(shards, S_DEV, width), SHARD, 0, 0, tiled=True)
+    other_queries = swap(queries)
+    shape = jax.ShapeDtypeStruct((width, queries.shape[0]), BF16)
+    q_own, q_other = call(query_kernel, [shape, shape], (queries, other_queries, w_query), flops=2**27)
     copies = normed_copies(arrived, ("z_hi", "z_lo", "y"))
     column = lax.all_to_all(copies, ("z_hi", "z_lo", "y"), 0, 0, tiled=True).reshape(-1, width)
-    near = spread(column, ("x",))
-    return attention(queries, near, w_query, w_key, w_value, w_out)
+    near = spread(column, ("x",)).reshape(-1, width)
+    return attention(q_own, q_other, near, w_key, w_value, w_out)
 
 
 def solution(mesh):

time: 77 us -> 78.6 us (1.021)
  blocking collectives: 59.7 us -> 47.9 us
  starting transfers between devices: 5.99 us -> 14.2 us
  local copies, waits for them, and re-layouts: 0.15 us -> 3.56 us
  waiting for transfers between devices: 0.01 us -> 2.59 us
  Pallas kernels: 10.8 us -> 9.8 us
    all_to_all x1 -> x0, blocking collectives: 11.8 us -> none  [spread(): lax.all_to_all(copies, axes, 0, 0, tiled=True).reshape(-1, rows.shape[-1])]
    ppermute x1 -> x2, starting transfers between devices: 5.99 us -> 10.6 us  [swap(): return lax.ppermute(rows, 'core', [(0, 1), (1, 0)])]
    all_to_all x0 -> x1, starting transfers between devices: none -> 3.62 us  [spread(): lax.all_to_all(copies, axes, 0, 0, tiled=True).reshape(-1, rows.shape[-1])]
    unnamed x10 -> x18, local copies, waits for them, and re-layouts: 0.03 us -> 2.53 us
    all_to_all x0 -> x1, waiting for transfers between devices: none -> 1.7 us  [spread(): lax.all_to_all(copies, axes, 0, 0, tiled=True).reshape(-1, rows.shape[-1])]
    broadcast_in_dim x2, local copies, waits for them, and re-layouts: 0.13 us -> 1.03 us  [spread(): copies = jnp.broadcast_to(rows[None], (count, *rows.shape))]
    ppermute x1 -> x2, waiting for transfers between devices: 0.01 us -> 0.88 us  [swap(): return lax.ppermute(rows, 'core', [(0, 1), (1, 0)])]
    pallas_call x2 -> x4, Pallas kernels: 7.43 us -> 6.73 us  [call(): pl.pallas_call(kernel, out_shape=shapes, in_specs=[VMEM] * len(operands),...]
  transfers between devices with their start and end apart: 1 -> 3, of which waited for: 0 -> 2; matrix products, arithmetic and copies ran while one was open for 0% -> 0% of each run, Pallas kernels for 4% -> 3%
where the time goes in v5:
time: 78.6 us; the launch traced here: 78.2 us
  blocking collectives  47.9 us (61%)
  starting transfers between devices  14.2 us (18%)
  Pallas kernels  9.8 us (12%)
  local copies, waits for them, and re-layouts  3.56 us (5%)
  waiting for transfers between devices  2.59 us (3%)
    all_to_all x1, blocking collectives, body(): lax.all_to_all(copies, ('z_hi', 'z_lo', 'y'), 0, 0, tiled=True)  24.2 us
    all_to_all x1, blocking collectives, body(): lax.all_to_all(partial.reshape(shards, S_DEV, width), SHARD, 0, 0, tiled=...  23.7 us
    ppermute x2, starting transfers between devices, swap(): return lax.ppermute(rows, 'core', [(0, 1), (1, 0)])  10.6 us
    pallas_call x4, Pallas kernels, call(): pl.pallas_call(kernel, out_shape=shapes, in_specs=[VMEM] * len(operands),...  6.73 us
    all_to_all x1, starting transfers between devices, spread(): lax.all_to_all(copies, axes, 0, 0, tiled=True).reshape(-1, rows.shape[-1])  3.62 us
    pallas_call x1, Pallas kernels, pool(): pl.pallas_call(functools.partial(pool_kernel, block_points), out_shape=ja...  2.69 us
    unnamed x18, local copies, waits for them, and re-layouts  2.53 us
    all_to_all x1, waiting for transfers between devices, spread(): lax.all_to_all(copies, axes, 0, 0, tiled=True).reshape(-1, rows.shape[-1])  1.7 us
  transfers between devices with their start and end apart: 3, of which 2 were waited for; matrix products, arithmetic and copies ran while one was open for 0% of the time, Pallas kernels for 3%

profile of v5, /device:TPU:1, one launch (start us, length us, event | category | flops | bytes accessed | tf_op | source)
XLA Modules:
  0.0 78.2 jit_solution(4545380062126563752)
XLA Ops:
  0.0 2.7 %pool.1 = bf16[64,2,768]{2,1,0:T(2,128)(2,1)} custom-call(s32[96]{0:T(128)} %bitcast.5, s32[96]{0:T(128)} %node_in.1, bf16[768,128]{1,0:T(8,128)(2,1)} %bitcast.4, bf16[128,768]{1,0:T(8,128)(2,1)} %w_in_in.1), custom_call_target="tpu_custom_call" | custom-call | flops 268435456 | bytes 1048576 | tf_op jit(solution)/shard_map/pool/pallas_call | solution.py:80
  2.7 23.7 %all_to_all.15.arrived = bf16[64,2,768]{2,1,0:T(2,128)(2,1)S(1)} all-to-all(bf16[64,2,768]{2,1,0:T(2,128)(2,1)} %pool.1), channel_id=1, replica_groups=mesh['z_hi'=4,'core'=2,'z_lo'=2,'x'=4,'y'=8] {'z_lo','x','y'}, dimensions={0} | all-to-all | bytes 393216 | tf_op jit(solution)/shard_map/all_to_all | solution.py:278
  26.4 0.4 norm.1
  26.8 24.2 %all_to_all.16 = bf16[64,2,768]{2,1,0:T(2,128)(2,1)S(1)} all-to-all(bf16[64,2,768]{2,1,0:T(2,128)(2,1)S(1)} %norm.1), channel_id=1, replica_groups=mesh['z_hi'=4,'core'=2,'z_lo'=2,'x'=4,'y'=8] {'z_hi','z_lo','y'}, dimensions={0} | all-to-all | bytes 393216 | tf_op jit(solution)/shard_map/all_to_all | solution.py:283
  51.0 0.1 broadcast_in_dim.7
  51.1 0.0 copy-start.4
  51.1 0.0 copy-start.3
  51.1 0.0 copy-start.2
  51.1 1.0 %broadcast_in_dim.8 = bf16[4,128,768]{2,1,0:T(8,128)(2,1)} broadcast(bf16[128,768]{1,0:T(8,128)(2,1)S(1)} %broadcast_in_dim.7), dimensions={1,2} | broadcast | bytes 983040 | tf_op jit(solution)/shard_map/broadcast_in_dim | solution.py:270
  52.1 0.0 copy-start.1
  52.1 3.6 %all-to-all-start.2 = ((bf16[4,128,768]{2,1,0:T(8,128)(2,1)}), bf16[4,128,768]{2,1,0:T(8,128)(2,1)S(1)}, u32[]{:S(2)}, u32[]{:S(2)}) async-start(bf16[4,128,768]{2,1,0:T(8,128)(2,1)} %broadcast_in_dim.8), calls=%async_computation.2 | async-start | bytes 1572864 | tf_op jit(solution)/shard_map/all_to_all | solution.py:271
  55.7 0.0 copy-done.4
  55.7 4.7 %collective-permute-start = (bf16[256,128]{1,0:T(8,128)(2,1)S(1)}, bf16[256,128]{1,0:T(8,128)(2,1)S(1)}, u32[]{:S(2)}, u32[]{:S(2)}) collective-permute-start(bf16[256,128]{1,0:T(8,128)(2,1)S(1)} %copy-done.4), channel_id=1, source_target_pairs={{0,64},{64,0},{1,65},{65,1},{2,66},{66,2},{3,67},{67,3},{4,68},{68... | collective-permute-start | bytes 196616 | tf_op jit(solution)/shard_map/ppermute | solution.py:218
  60.4 0.9 %collective-permute-done.other_queries = bf16[256,128]{1,0:T(8,128)(2,1)S(1)} collective-permute-done((bf16[256,128]{1,0:T(8,128)(2,1)S(1)}, bf16[256,128]{1,0:T(8,128)(2,1)S(1)}, u32[]{:S(2)}, u32[]{:S(2)}) %collective-permute-start) | collective-permute-done | bytes 65568 | tf_op jit(solution)/shard_map/ppermute | solution.py:218
  61.3 0.0 copy-done.3
  61.3 0.4 shard_map.91
  61.7 0.0 copy-start.5
  61.7 0.7 copy-done.5
  62.5 0.0 copy-start.7
  62.5 0.8 copy-done.7
  63.2 1.7 %all-to-all-done.2 = bf16[4,128,768]{2,1,0:T(8,128)(2,1)S(1)} async-done(((bf16[4,128,768]{2,1,0:T(8,128)(2,1)}), bf16[4,128,768]{2,1,0:T(8,128)(2,1)S(1)}, u32[]{:S(2)}, u32[]{:S(2)}) %all-to-all-start.2) | async-done | bytes 786464 | tf_op jit(solution)/shard_map/all_to_all | solution.py:271
  64.9 0.0 copy-done.2
  64.9 0.0 copy-done.1
  64.9 0.0 copy-start.8
  64.9 1.0 %copy-done.8 = bf16[768,256]{1,0:T(8,128)(2,1)S(1)} copy-done((bf16[768,256]{1,0:T(8,128)(2,1)S(1)}, bf16[768,256]{1,0:T(8,128)(2,1)}, u32[]{:S(2)}) %copy-start.8) | copy-done | bytes 393240
  65.9 0.0 copy-start.6
  65.9 3.2 %shard_map.92 = (bf16[512,768]{1,0:T(8,128)(2,1)S(1)}, bf16[768,512]{1,0:T(8,128)(2,1)S(1)}, bf16[864,256]{1,0:T(8,128)(2,1)S(1)}) custom-call(bf16[768,256]{1,0:T(8,128)(2,1)S(1)} %copy-done.8, bf16[512,768]{1,0:T(8,128)(2,1)S(1)} %bitcast.3, bf16[768,768]{1,0:T(8,128)(2,1)S(1)} %copy-done.1, bf16[768,768]{1,0:T(8,128)(2,1)S(1)} %copy-done.2), custom_call_target="tpu_custom_call" | custom-call | flops 3221225472 | bytes 1048576 | tf_op jit(solution)/shard_map/pallas_call | solution.py:206
  69.1 5.9 %collective-permute-start.1 = (bf16[864,256]{1,0:T(8,128)(2,1)S(1)}, bf16[864,256]{1,0:T(8,128)(2,1)S(1)}, u32[]{:S(2)}, u32[]{:S(2)}) collective-permute-start(bf16[864,256]{1,0:T(8,128)(2,1)S(1)} %get-tuple-element.18), channel_id=1, source_target_pairs={{0,64},{64,0},{1,65},{65,1},{2,66},{66,2},{3,67},{67,3},{4,68},{68... | collective-permute-start | bytes 1327112 | tf_op jit(solution)/shard_map/ppermute | solution.py:218
  75.0 0.0 copy-done.6
  75.0 0.0 copy-start
  75.0 2.2 %shard_map.93 = (f32[24,256]{1,0:T(8,128)S(1)}, f32[768,256]{1,0:T(8,128)S(1)}) custom-call(bf16[768,256]{1,0:T(8,128)(2,1)S(1)} %copy-done.6, bf16[512,768]{1,0:T(8,128)(2,1)S(1)} %get-tuple-element.14.keys, bf16[768,512]{1,0:T(8,128)(2,1)S(1)} %get-tuple-element.15.values), custom_call_target="tpu_custom_call" | custom-call | flops 1610612736 | bytes 1048576 | tf_op jit(solution)/shard_map/pallas_call | solution.py:206
  77.2 0.0 collective-permute-done.1.given
  77.2 0.0 copy-done
  77.2 1.0 %shard_map.94 = bf16[256,128]{1,0:T(8,128)(2,1)} custom-call(f32[24,256]{1,0:T(8,128)S(1)} %get-tuple-element.16.stats, f32[768,256]{1,0:T(8,128)S(1)} %get-tuple-element.17.summed, bf16[864,256]{1,0:T(8,128)(2,1)S(1)} %collective-permute-done.1.given, bf16[768,128]{1,0:T(8,128)(2,1)S(1)} %copy-done), custom_call_target="tpu_custom_call" | custom-call | bytes 1048576 | tf_op jit(solution)/shard_map/pallas_call | solution.py:206
Async XLA Ops:
  51.1 4.6 %copy-start.4 = (bf16[256,128]{1,0:T(8,128)(2,1)S(1)}, bf16[256,128]{1,0:T(8,128)(2,1)}, u32[]{:S(2)}) copy-start(bf16[256,128]{1,0:T(8,128)(2,1)} %queries.1) | copy-start | bytes 196612
  51.1 10.2 %copy-start.3 = (bf16[128,768]{1,0:T(8,128)(2,1)S(1)}, bf16[128,768]{1,0:T(8,128)(2,1)}, u32[]{:S(2)}) copy-start(bf16[128,768]{1,0:T(8,128)(2,1)} %w_query.1) | copy-start | bytes 589828
  51.1 13.8 %copy-start.2 = (bf16[768,768]{1,0:T(8,128)(2,1)S(1)}, bf16[768,768]{1,0:T(8,128)(2,1)}, u32[]{:S(2)}) copy-start(bf16[768,768]{1,0:T(8,128)(2,1)} %w_value.1) | copy-start | bytes 3538948
  52.1 12.9 %copy-start.1 = (bf16[768,768]{1,0:T(8,128)(2,1)S(1)}, bf16[768,768]{1,0:T(8,128)(2,1)}, u32[]{:S(2)}) copy-start(bf16[768,768]{1,0:T(8,128)(2,1)} %w_key.1) | copy-start | bytes 3538948
  52.1 12.9 %all-to-all-start.2 = ((bf16[4,128,768]{2,1,0:T(8,128)(2,1)}), bf16[4,128,768]{2,1,0:T(8,128)(2,1)S(1)}, u32[]{:S(2)}, u32[]{:S(2)}) async-start(bf16[4,128,768]{2,1,0:T(8,128)(2,1)} %broadcast_in_dim.8), calls=%async_computation.2 | async-start | bytes 1572864 | tf_op jit(solution)/shard_map/all_to_all | solution.py:271
  55.7 5.6 %collective-permute-start = (bf16[256,128]{1,0:T(8,128)(2,1)S(1)}, bf16[256,128]{1,0:T(8,128)(2,1)S(1)}, u32[]{:S(2)}, u32[]{:S(2)}) collective-permute-start(bf16[256,128]{1,0:T(8,128)(2,1)S(1)} %copy-done.4), channel_id=1, source_target_pairs={{0,64},{64,0},{1,65},{65,1},{2,66},{66,2},{3,67},{67,3},{4,68},{68... | collective-permute-start | bytes 196616 | tf_op jit(solution)/shard_map/ppermute | solution.py:218
  61.7 0.7 copy-start.5
  62.5 0.8 copy-start.7
  64.9 1.0 %copy-start.8 = (bf16[768,256]{1,0:T(8,128)(2,1)S(1)}, bf16[768,256]{1,0:T(8,128)(2,1)}, u32[]{:S(2)}) copy-start(bf16[768,256]{1,0:T(8,128)(2,1)} %copy-done.7) | copy-start | bytes 1179652
  65.9 9.1 %copy-start.6 = (bf16[768,256]{1,0:T(8,128)(2,1)S(1)}, bf16[768,256]{1,0:T(8,128)(2,1)}, u32[]{:S(2)}) copy-start(bf16[768,256]{1,0:T(8,128)(2,1)} %copy-done.5) | copy-start | bytes 1179652
  69.1 8.1 %collective-permute-start.1 = (bf16[864,256]{1,0:T(8,128)(2,1)S(1)}, bf16[864,256]{1,0:T(8,128)(2,1)S(1)}, u32[]{:S(2)}, u32[]{:S(2)}) collective-permute-start(bf16[864,256]{1,0:T(8,128)(2,1)S(1)} %get-tuple-element.18), channel_id=1, source_target_pairs={{0,64},{64,0},{1,65},{65,1},{2,66},{66,2},{3,67},{67,3},{4,68},{68... | collective-permute-start | bytes 1327112 | tf_op jit(solution)/shard_map/ppermute | solution.py:218
  75.0 2.2 %copy-start = (bf16[768,128]{1,0:T(8,128)(2,1)S(1)}, bf16[768,128]{1,0:T(8,128)(2,1)}, u32[]{:S(2)}) copy-start(bf16[768,128]{1,0:T(8,128)(2,1)} %w_out.1) | copy-start | bytes 589828

commit v6 on v5

--- a/solution.py
+++ b/solution.py
@@ -16,6 +16,8 @@
 GELU_B = 4 * 0.044715 * GELU_A
 AXES = ("z_hi", "core", "z_lo", "x", "y")
 SHARD = ("z_lo", "x", "y")
+EXCHANGE = ("x", "z_lo", "y")
+COLUMN = ("z_lo", "y", "z_hi")
 BF16 = jnp.bfloat16
 F32 = jnp.float32
 PAIR = 2 * HEAD_DIM
@@ -36,7 +38,7 @@
     return lax.dot_general(a, b, (dims, ((), ())), preferred_element_type=F32)
 
 
-def pool_kernel(block_points, owner_in, node_in, points_in, w_in_in, out, owner, node, points, w_in, pick, sems):
+def pool_kernel(block_points, sizes, owner_in, node_in, points_in, w_in_in, out, owner, node, points, w_in, pick, sems):
     pairs = ((owner_in, owner), (node_in, node), (w_in_in, w_in), (points_in, points))
     copies = [pltpu.make_async_copy(a, b, sems.at[i]) for i, (a, b) in enumerate(pairs)]
     for copy in copies:
@@ -44,6 +46,11 @@
     blocks, slots = owner.shape[0], pick.shape[1]
     rows = 2 * block_points
     lane = lax.broadcasted_iota(jnp.int32, (rows, slots), 1)
+    place, lane = lane // S_DEV, lane % S_DEV
+    for axis in reversed(EXCHANGE):
+        later = SHARD[SHARD.index(axis) + 1 :]
+        lane = lane + place % sizes[axis] * (S_DEV * math.prod(sizes[a] for a in later))
+        place = place // sizes[axis]
     first = lax.broadcasted_iota(jnp.int32, (rows, slots), 0) < block_points
     copies[0].wait()
     copies[1].wait()
@@ -78,7 +85,7 @@
     blocks, block_points, features = points.shape
     rows = blocks * block_points
     return pl.pallas_call(
-        functools.partial(pool_kernel, block_points),
+        functools.partial(pool_kernel, block_points, {a: lax.axis_size(a) for a in SHARD}),
         out_shape=jax.ShapeDtypeStruct((slots // S_DEV, S_DEV, w_in.shape[1]), BF16),
         in_specs=[HBM] * 4,
         out_specs=VMEM,
@@ -275,12 +282,12 @@
     shards = lax.axis_size(SHARD)
     width = w_in.shape[1]
     partial = pool(points, block_owner[:, 0], block_node, w_in, shards * S_DEV)
-    arrived = lax.all_to_all(partial.reshape(shards, S_DEV, width), SHARD, 0, 0, tiled=True)
+    arrived = lax.all_to_all(partial.reshape(shards, S_DEV, width), EXCHANGE, 0, 0, tiled=True)
     other_queries = swap(queries)
     shape = jax.ShapeDtypeStruct((width, queries.shape[0]), BF16)
     q_own, q_other = call(query_kernel, [shape, shape], (queries, other_queries, w_query), flops=2**27)
-    copies = normed_copies(arrived, ("z_hi", "z_lo", "y"))
-    column = lax.all_to_all(copies, ("z_hi", "z_lo", "y"), 0, 0, tiled=True).reshape(-1, width)
+    copies = normed_copies(arrived, COLUMN)
+    column = lax.all_to_all(copies, COLUMN, 0, 0, tiled=True).reshape(-1, width)
     near = spread(column, ("x",)).reshape(-1, width)
     return attention(q_own, q_other, near, w_key, w_value, w_out)
 

time: 78.6 us -> 76.6 us (0.975)
  blocking collectives: 47.9 us -> 45.9 us
  starting transfers between devices: 14.2 us -> 15.4 us
  waiting for transfers between devices: 2.59 us -> 1.44 us
    all_to_all x2, blocking collectives: 47.9 us -> 45.9 us  [the longest x1 23.8 us: body(): lax.all_to_all(partial.reshape(shards, S_DEV, width), EXCHANGE, 0, 0, til...]
    ppermute x2, starting transfers between devices: 10.6 us -> 11.8 us  [swap(): return lax.ppermute(rows, 'core', [(0, 1), (1, 0)])]
    all_to_all x1, waiting for transfers between devices: 1.7 us -> 0.56 us  [spread(): lax.all_to_all(copies, axes, 0, 0, tiled=True).reshape(-1, rows.shape[-1])]
where the time goes in v6:
time: 76.6 us; the launch traced here: 76.2 us
  blocking collectives  45.9 us (60%)
  starting transfers between devices  15.4 us (20%)
  Pallas kernels  9.8 us (13%)
  local copies, waits for them, and re-layouts  3.56 us (5%)
  waiting for transfers between devices  1.44 us (2%)
    all_to_all x1, blocking collectives, body(): lax.all_to_all(partial.reshape(shards, S_DEV, width), EXCHANGE, 0, 0, til...  23.8 us
    all_to_all x1, blocking collectives, body(): column = lax.all_to_all(copies, COLUMN, 0, 0, tiled=True).reshape(-1, width)  22.1 us
    ppermute x2, starting transfers between devices, swap(): return lax.ppermute(rows, 'core', [(0, 1), (1, 0)])  11.8 us
    pallas_call x4, Pallas kernels, call(): pl.pallas_call(kernel, out_shape=shapes, in_specs=[VMEM] * len(operands),...  6.73 us
    all_to_all x1, starting transfers between devices, spread(): lax.all_to_all(copies, axes, 0, 0, tiled=True).reshape(-1, rows.shape[-1])  3.62 us
    pallas_call x1, Pallas kernels, pool(): pl.pallas_call(functools.partial(pool_kernel, block_points, {a: lax.axis_...  2.69 us
    unnamed x18, local copies, waits for them, and re-layouts  2.53 us
  transfers between devices with their start and end apart: 3, of which 2 were waited for; matrix products, arithmetic and copies ran while one was open for 0% of the time, Pallas kernels for 3%

profile of v6, /device:TPU:1, one launch (start us, length us, event | category | flops | bytes accessed | tf_op | source)
XLA Modules:
  0.0 76.2 jit_solution(5793766752594270690)
XLA Ops:
  0.0 2.7 %pool.1 = bf16[64,2,768]{2,1,0:T(2,128)(2,1)} custom-call(s32[96]{0:T(128)} %bitcast.5, s32[96]{0:T(128)} %node_in.1, bf16[768,128]{1,0:T(8,128)(2,1)} %bitcast.4, bf16[128,768]{1,0:T(8,128)(2,1)} %w_in_in.1), custom_call_target="tpu_custom_call" | custom-call | flops 268435456 | bytes 1048576 | tf_op jit(solution)/shard_map/pool/pallas_call | solution.py:87
  2.7 23.8 %all_to_all.15.arrived = bf16[64,2,768]{2,1,0:T(2,128)(2,1)S(1)} all-to-all(bf16[64,2,768]{2,1,0:T(2,128)(2,1)} %pool.1), channel_id=1, replica_groups=mesh['z_hi'=4,'core'=2,'z_lo'=2,'x'=4,'y'=8] {'x','z_lo','y'}, dimensions={0} | all-to-all | bytes 393216 | tf_op jit(solution)/shard_map/all_to_all | solution.py:285
  26.5 0.4 norm.1
  26.9 22.1 %all_to_all.16 = bf16[64,2,768]{2,1,0:T(2,128)(2,1)S(1)} all-to-all(bf16[64,2,768]{2,1,0:T(2,128)(2,1)S(1)} %norm.1), channel_id=1, replica_groups=mesh['z_hi'=4,'core'=2,'z_lo'=2,'x'=4,'y'=8] {'z_lo','y','z_hi'}, dimensions={0} | all-to-all | bytes 393216 | tf_op jit(solution)/shard_map/all_to_all | solution.py:290
  49.0 0.1 broadcast_in_dim.7
  49.1 0.0 copy-start.4
  49.1 0.0 copy-start.3
  49.1 0.0 copy-start.2
  49.1 1.0 %broadcast_in_dim.8 = bf16[4,128,768]{2,1,0:T(8,128)(2,1)} broadcast(bf16[128,768]{1,0:T(8,128)(2,1)S(1)} %broadcast_in_dim.7), dimensions={1,2} | broadcast | bytes 983040 | tf_op jit(solution)/shard_map/broadcast_in_dim | solution.py:277
  50.1 0.0 copy-start.1
  50.1 3.6 %all-to-all-start.2 = ((bf16[4,128,768]{2,1,0:T(8,128)(2,1)}), bf16[4,128,768]{2,1,0:T(8,128)(2,1)S(1)}, u32[]{:S(2)}, u32[]{:S(2)}) async-start(bf16[4,128,768]{2,1,0:T(8,128)(2,1)} %broadcast_in_dim.8), calls=%async_computation.2 | async-start | bytes 1572864 | tf_op jit(solution)/shard_map/all_to_all | solution.py:278
  53.7 0.0 copy-done.4
  53.7 5.3 %collective-permute-start = (bf16[256,128]{1,0:T(8,128)(2,1)S(1)}, bf16[256,128]{1,0:T(8,128)(2,1)S(1)}, u32[]{:S(2)}, u32[]{:S(2)}) collective-permute-start(bf16[256,128]{1,0:T(8,128)(2,1)S(1)} %copy-done.4), channel_id=1, source_target_pairs={{0,64},{64,0},{1,65},{65,1},{2,66},{66,2},{3,67},{67,3},{4,68},{68... | collective-permute-start | bytes 196616 | tf_op jit(solution)/shard_map/ppermute | solution.py:225
  59.0 0.9 %collective-permute-done.other_queries = bf16[256,128]{1,0:T(8,128)(2,1)S(1)} collective-permute-done((bf16[256,128]{1,0:T(8,128)(2,1)S(1)}, bf16[256,128]{1,0:T(8,128)(2,1)S(1)}, u32[]{:S(2)}, u32[]{:S(2)}) %collective-permute-start) | collective-permute-done | bytes 65568 | tf_op jit(solution)/shard_map/ppermute | solution.py:225
  59.9 0.0 copy-done.3
  59.9 0.4 shard_map.91
  60.3 0.0 copy-start.5
  60.3 0.7 copy-done.5
  61.0 0.0 copy-start.7
  61.0 0.8 copy-done.7
  61.8 0.6 all-to-all-done.2
  62.4 0.0 copy-done.2
  62.4 0.0 copy-done.1
  62.4 0.0 copy-start.8
  62.4 1.0 %copy-done.8 = bf16[768,256]{1,0:T(8,128)(2,1)S(1)} copy-done((bf16[768,256]{1,0:T(8,128)(2,1)S(1)}, bf16[768,256]{1,0:T(8,128)(2,1)}, u32[]{:S(2)}) %copy-start.8) | copy-done | bytes 393240
  63.4 0.0 copy-start.6
  63.4 3.2 %shard_map.92 = (bf16[512,768]{1,0:T(8,128)(2,1)S(1)}, bf16[768,512]{1,0:T(8,128)(2,1)S(1)}, bf16[864,256]{1,0:T(8,128)(2,1)S(1)}) custom-call(bf16[768,256]{1,0:T(8,128)(2,1)S(1)} %copy-done.8, bf16[512,768]{1,0:T(8,128)(2,1)S(1)} %bitcast.3, bf16[768,768]{1,0:T(8,128)(2,1)S(1)} %copy-done.1, bf16[768,768]{1,0:T(8,128)(2,1)S(1)} %copy-done.2), custom_call_target="tpu_custom_call" | custom-call | flops 3221225472 | bytes 1048576 | tf_op jit(solution)/shard_map/pallas_call | solution.py:213
  66.6 6.5 %collective-permute-start.1 = (bf16[864,256]{1,0:T(8,128)(2,1)S(1)}, bf16[864,256]{1,0:T(8,128)(2,1)S(1)}, u32[]{:S(2)}, u32[]{:S(2)}) collective-permute-start(bf16[864,256]{1,0:T(8,128)(2,1)S(1)} %get-tuple-element.18), channel_id=1, source_target_pairs={{0,64},{64,0},{1,65},{65,1},{2,66},{66,2},{3,67},{67,3},{4,68},{68... | collective-permute-start | bytes 1327112 | tf_op jit(solution)/shard_map/ppermute | solution.py:225
  73.0 0.0 copy-done.6
  73.0 0.0 copy-start
  73.0 2.2 %shard_map.93 = (f32[24,256]{1,0:T(8,128)S(1)}, f32[768,256]{1,0:T(8,128)S(1)}) custom-call(bf16[768,256]{1,0:T(8,128)(2,1)S(1)} %copy-done.6, bf16[512,768]{1,0:T(8,128)(2,1)S(1)} %get-tuple-element.14.keys, bf16[768,512]{1,0:T(8,128)(2,1)S(1)} %get-tuple-element.15.values), custom_call_target="tpu_custom_call" | custom-call | flops 1610612736 | bytes 1048576 | tf_op jit(solution)/shard_map/pallas_call | solution.py:213
  75.2 0.0 collective-permute-done.1.given
  75.2 0.0 copy-done
  75.2 1.0 %shard_map.94 = bf16[256,128]{1,0:T(8,128)(2,1)} custom-call(f32[24,256]{1,0:T(8,128)S(1)} %get-tuple-element.16.stats, f32[768,256]{1,0:T(8,128)S(1)} %get-tuple-element.17.summed, bf16[864,256]{1,0:T(8,128)(2,1)S(1)} %collective-permute-done.1.given, bf16[768,128]{1,0:T(8,128)(2,1)S(1)} %copy-done), custom_call_target="tpu_custom_call" | custom-call | bytes 1048576 | tf_op jit(solution)/shard_map/pallas_call | solution.py:213
Async XLA Ops:
  49.1 4.6 %copy-start.4 = (bf16[256,128]{1,0:T(8,128)(2,1)S(1)}, bf16[256,128]{1,0:T(8,128)(2,1)}, u32[]{:S(2)}) copy-start(bf16[256,128]{1,0:T(8,128)(2,1)} %queries.1) | copy-start | bytes 196612
  49.1 10.8 %copy-start.3 = (bf16[128,768]{1,0:T(8,128)(2,1)S(1)}, bf16[128,768]{1,0:T(8,128)(2,1)}, u32[]{:S(2)}) copy-start(bf16[128,768]{1,0:T(8,128)(2,1)} %w_query.1) | copy-start | bytes 589828
  49.1 13.3 %copy-start.2 = (bf16[768,768]{1,0:T(8,128)(2,1)S(1)}, bf16[768,768]{1,0:T(8,128)(2,1)}, u32[]{:S(2)}) copy-start(bf16[768,768]{1,0:T(8,128)(2,1)} %w_value.1) | copy-start | bytes 3538948
  50.1 12.3 %copy-start.1 = (bf16[768,768]{1,0:T(8,128)(2,1)S(1)}, bf16[768,768]{1,0:T(8,128)(2,1)}, u32[]{:S(2)}) copy-start(bf16[768,768]{1,0:T(8,128)(2,1)} %w_key.1) | copy-start | bytes 3538948
  50.1 12.3 %all-to-all-start.2 = ((bf16[4,128,768]{2,1,0:T(8,128)(2,1)}), bf16[4,128,768]{2,1,0:T(8,128)(2,1)S(1)}, u32[]{:S(2)}, u32[]{:S(2)}) async-start(bf16[4,128,768]{2,1,0:T(8,128)(2,1)} %broadcast_in_dim.8), calls=%async_computation.2 | async-start | bytes 1572864 | tf_op jit(solution)/shard_map/all_to_all | solution.py:278
  53.7 6.2 %collective-permute-start = (bf16[256,128]{1,0:T(8,128)(2,1)S(1)}, bf16[256,128]{1,0:T(8,128)(2,1)S(1)}, u32[]{:S(2)}, u32[]{:S(2)}) collective-permute-start(bf16[256,128]{1,0:T(8,128)(2,1)S(1)} %copy-done.4), channel_id=1, source_target_pairs={{0,64},{64,0},{1,65},{65,1},{2,66},{66,2},{3,67},{67,3},{4,68},{68... | collective-permute-start | bytes 196616 | tf_op jit(solution)/shard_map/ppermute | solution.py:225
  60.3 0.7 copy-start.5
  61.0 0.8 %copy-start.7 = (bf16[768,256]{1,0:T(8,128)(2,1)}, bf16[768,256]{1,0:T(8,128)(2,1)S(1)}, u32[]{:S(2)}) copy-start(bf16[768,256]{1,0:T(8,128)(2,1)S(1)} %get-tuple-element.13.q_cols) | copy-start | bytes 1179652
  62.4 1.0 %copy-start.8 = (bf16[768,256]{1,0:T(8,128)(2,1)S(1)}, bf16[768,256]{1,0:T(8,128)(2,1)}, u32[]{:S(2)}) copy-start(bf16[768,256]{1,0:T(8,128)(2,1)} %copy-done.7) | copy-start | bytes 1179652
  63.4 9.7 %copy-start.6 = (bf16[768,256]{1,0:T(8,128)(2,1)S(1)}, bf16[768,256]{1,0:T(8,128)(2,1)}, u32[]{:S(2)}) copy-start(bf16[768,256]{1,0:T(8,128)(2,1)} %copy-done.5) | copy-start | bytes 1179652
  66.6 8.7 %collective-permute-start.1 = (bf16[864,256]{1,0:T(8,128)(2,1)S(1)}, bf16[864,256]{1,0:T(8,128)(2,1)S(1)}, u32[]{:S(2)}, u32[]{:S(2)}) collective-permute-start(bf16[864,256]{1,0:T(8,128)(2,1)S(1)} %get-tuple-element.18), channel_id=1, source_target_pairs={{0,64},{64,0},{1,65},{65,1},{2,66},{66,2},{3,67},{67,3},{4,68},{68... | collective-permute-start | bytes 1327112 | tf_op jit(solution)/shard_map/ppermute | solution.py:225
  73.0 2.2 %copy-start = (bf16[768,128]{1,0:T(8,128)(2,1)S(1)}, bf16[768,128]{1,0:T(8,128)(2,1)}, u32[]{:S(2)}) copy-start(bf16[768,128]{1,0:T(8,128)(2,1)} %w_out.1) | copy-start | bytes 589828
